TPU v7x, 32 devices: a whole 2x2x4 slice. The times are simulated.
32 devices in a mesh: rep: 2 (over y), tract: 4 (over x, core), head: 4 (over z).
Axes of the slice: x: 2, y: 2, z: 4, core: 2. Of those that a mesh axis runs over, the one named last changes fastest.
Arguments:
- frames: bfloat16 [8, 256, 6144], P(('rep', 'tract'), 'head'), parts along dimension 0, may hold values from -7 to 7
- levels: int32 [8], P(('rep', 'tract')), parts along dimension 0, may hold values from 0 to 7
- visible: int32 [8, 4], P(('rep', 'tract')), parts along dimension 0, may hold values from 0 to 1, as said below
- w_qkv: bfloat16 [6144, 3, 1024], P(None, None, 'head'), may hold values from -0.2 to 0.2
- w_out: bfloat16 [1024, 6144], P('head'), may hold values from -1.5 to 1.5
- modulation: float32 [8, 3, 6144], replicated, may hold values from -3 to 3
Outputs:
- mixed: bfloat16 [8, 256, 6144], P(('rep', 'tract'), 'head'), parts along dimension 0
There are 2 independent parts, one for each index of `rep`. A program takes and returns all parts, laid end to end along the dimension named above; an argument that names none is the same for every part. Nothing has to cross between parts.
Inputs may be any that keep to these rules, and one draw needn't show every extreme that they name: visible[c, c] is 1 and visible[c, j] is 0 for every j > c.
All inputs are finite; a program needn't handle non-finite values.
Results may differ from a plain program's by a relative error of at most 0.019.
Values may be sent and summed in bfloat16 or wider, within the bound.
A program may use at most 64 MiB of HBM per device.

v0:
```python
import functools

import jax
import jax.numpy as jnp
from jax import lax
from jax.experimental import pallas as pl
from jax.experimental.pallas import tpu as pltpu
from jax.sharding import PartitionSpec as P

HD = 128
GRANT = 60 * 1024 * 1024
MESH = pl.DeviceIdType.MESH


def meet(n, me, tracts, tract, others):
    barrier = pltpu.get_barrier_semaphore()
    for other in (lax.rem(me + 1, n), lax.rem(me + n - 1, n)):
        pl.semaphore_signal(barrier, inc=1, device_id={"head": other}, device_id_type=MESH)
    for ahead in range(1, tracts):
        other = lax.rem(tract + ahead, tracts)
        pl.semaphore_signal(barrier, inc=1, device_id={"tract": other}, device_id_type=MESH)
    for other in others:
        pl.semaphore_signal(barrier, inc=1, device_id=other, device_id_type=MESH)
    pl.semaphore_wait(barrier, 1 + tracts + len(others))


def sublayer_kernel(
    n,
    tracts,
    reps,
    pieces,
    halves,
    x_ref,
    level_ref,
    visible_ref,
    w_hbm,
    out_hbm,
    table_ref,
    out_ref,
    got,
    wq_ref,
    w_ref,
    q_ref,
    kv_ref,
    kv_in,
    att_ref,
    peak_ref,
    sum_ref,
    acc_ref,
    going,
    landed,
    total_ref,
    load_sem,
    g_send,
    g_recv,
    kv_send,
    kv_recv,
    s_send,
    s_recv,
    w_far,
    att_far,
    f_send,
    f_recv,
):
    me, tract = lax.axis_index("head"), lax.axis_index("tract")
    own = pltpu.make_async_copy(x_ref.at[0], got.at[me], load_sem.at[0])
    own.start()
    load = pltpu.make_async_copy(w_hbm, wq_ref, load_sem.at[1])
    load.start()
    load_out = pltpu.make_async_copy(out_hbm, w_ref, load_sem.at[2])
    load_out.start()
    core, wide = tract % 2, tracts // 2
    chips = wide * reps
    chip = lax.axis_index("rep") * wide + tract // 2
    slab = w_ref.shape[0] // (2 * chips)
    helper = (me == 1) | (me == n - 2)
    ends = (me == 0) | (me == n - 1)

    def seat(by):
        other = lax.rem(chip + by, chips)
        return {"rep": other // wide, "tract": lax.rem(other, wide) * 2 + core}

    def slab_of(which, side):
        start = pl.multiple_of((which * 2 + side) * slab, slab)
        return pl.ds(start, slab)

    def far_copy(kind, span, target, source=None):
        return pltpu.make_async_remote_copy(
            src_ref=(w_far if source is None else source).at[span],
            dst_ref=w_far.at[span],
            send_sem=f_send.at[kind],
            recv_sem=f_recv.at[kind],
            device_id=target,
            device_id_type=MESH,
        )

    inward = {"head": jnp.where(me == 0, 1, n - 2)}
    partner = {"tract": tract + 1 - 2 * core}
    mine = slab_of(chip, core)

    def to_helper():
        return far_copy(0, mine, inward, out_hbm)

    def to_chip(by):
        return far_copy(by, mine, seat(by))

    def from_chip(by):
        return far_copy(by, slab_of(lax.rem(chip + chips - by, chips), core), seat(by))

    def to_partner(by):
        span = slab_of(lax.rem(chip + chips - by, chips), core)
        return far_copy(chips + by, span, partner)

    def from_partner(by):
        span = slab_of(lax.rem(chip + chips - by, chips), 1 - core)
        return far_copy(chips + by, span, partner)

    def att_copy():
        return pltpu.make_async_remote_copy(
            src_ref=att_ref,
            dst_ref=att_far,
            send_sem=f_send.at[2 * chips],
            recv_sem=f_recv.at[2 * chips],
            device_id=inward,
            device_id_type=MESH,
        )

    meet(n, me, tracts, tract, [seat(by) for by in range(1, chips)])
    level = level_ref[0]

    def style(kind):
        return table_ref[kind, pl.ds(level, 1), :]

    rows, width = x_ref.shape[1:]
    part = rows // pieces

    def copy(way, step, piece, first=False):
        side = (way + 1) // 2
        span = pl.ds(piece * part, part)
        block = me - way * step
        return pltpu.make_async_remote_copy(
            src_ref=(x_ref.at[0] if first else got.at[block]).at[span],
            dst_ref=got.at[block].at[span],
            send_sem=g_send.at[side, step, piece],
            recv_sem=g_recv.at[side, step, piece],
            device_id={"head": me + way},
            device_id_type=MESH,
        )

    def arrival(way, step, piece):
        side = (way + 1) // 2
        span = pl.ds(piece * part, part)
        return pltpu.make_async_remote_copy(
            src_ref=x_ref.at[0].at[span],
            dst_ref=got.at[me - way * (step + 1)].at[span],
            send_sem=g_send.at[side, step, piece],
            recv_sem=g_recv.at[side, step, piece],
            device_id={"head": me - way},
            device_id_type=MESH,
        )

    def sends(way, step):
        block, target = me - way * step, me + way
        return (block >= 0) & (block < n) & (target >= 0) & (target < n) & (step < n - 1)

    def receives(way, step):
        block = me - way * (step + 1)
        return (block >= 0) & (block < n)

    def kv_copy(ahead, block):
        return pltpu.make_async_remote_copy(
            src_ref=kv_ref.at[block],
            dst_ref=kv_in.at[ahead - 1, block],
            send_sem=kv_send.at[ahead - 1, block],
            recv_sem=kv_recv.at[ahead - 1, block],
            device_id={"tract": tract + ahead},
            device_id_type=MESH,
        )

    def project(block):
        tokens = got[block].astype(jnp.float32)
        power = jnp.mean(tokens * tokens, axis=-1, keepdims=True)
        normed = tokens * lax.rsqrt(power + 1e-06)
        shaped = (normed * (1.0 + style(1)) + style(0)).astype(jnp.bfloat16)
        for kind in (1, 2, 0):
            made = jnp.dot(shaped, wq_ref[kind], preferred_element_type=jnp.float32)
            made = made.astype(jnp.bfloat16)
            if kind == 0:
                q_ref[block] = made
            else:
                kv_ref[block, kind - 1] = made
            if kind == 2:
                for ahead in range(1, tracts):

                    @pl.when(tract + ahead < tracts)
                    def _():
                        kv_copy(ahead, block).start()

    for piece in range(pieces):
        for way in (-1, 1):

            @pl.when(sends(way, 0))
            def _():
                copy(way, 0, piece, True).start()

    @pl.when(ends)
    def _():
        to_helper().start()

    own.wait()
    load.wait()
    project(me)

    @pl.loop(0, n - 1)
    def _(step):
        for piece in range(pieces):
            for way in (-1, 1):

                @pl.when(receives(way, step))
                def _():
                    arrival(way, step, piece).wait_recv()

                @pl.when(sends(way, step + 1))
                def _():
                    copy(way, step + 1, piece).start()

        @pl.loop(0, 2)
        def _(side):
            way = 2 * side - 1

            @pl.when(receives(way, step))
            def _():
                project(me - way * (step + 1))

        @pl.when(helper & (step == 0))
        def _():
            to_helper().wait_recv()
            for by in range(1, chips):
                to_chip(by).start()
            to_partner(0).start()

    @pl.when(helper)
    def _():
        for by in range(1, chips):
            from_chip(by).wait_recv()
            to_partner(by).start()

    tokens_here = n * rows
    heads_here = q_ref.shape[2] // HD
    scale = HD ** (-0.5)

    def attend(source, allowed):
        for head in range(heads_here):
            lanes = slice(head * HD, (head + 1) * HD)
            queries = q_ref[:, :, lanes].reshape(tokens_here, HD)
            keys = source[:, 0, :, lanes].reshape(tokens_here, HD)
            values = source[:, 1, :, lanes].reshape(tokens_here, HD)
            scores = (
                lax.dot_general(
                    queries, keys, (((1,), (1,)), ((), ())), preferred_element_type=jnp.float32
                )
                * scale
            )
            if allowed is None:
                peak = jnp.max(scores, axis=1, keepdims=True)
                probs = jnp.exp(scores - peak)
            else:
                scores = jnp.where(allowed, scores, -1e30)
                old = peak_ref[head]
                peak = jnp.maximum(old, jnp.max(scores, axis=1, keepdims=True))
                probs = jnp.where(allowed, jnp.exp(scores - peak), 0.0)
                rescale = jnp.exp(old - peak)
            row_sum = jnp.sum(probs, axis=1, keepdims=True)
            weighted = jnp.dot(
                probs.astype(jnp.bfloat16), values, preferred_element_type=jnp.float32
            )
            if allowed is not None:
                row_sum += sum_ref[head] * rescale
                weighted += acc_ref[head] * rescale
            peak_ref[head] = peak
            sum_ref[head] = row_sum
            acc_ref[head] = weighted

    attend(kv_ref, None)
    for ahead in range(1, tracts):

        @pl.when(tract >= ahead)
        def _():
            @pl.loop(0, n)
            def _(block):
                kv_copy(ahead, block).wait_recv()

            attend(kv_in.at[ahead - 1], visible_ref[0, lax.max(tract - ahead, 0)] > 0)

    for head in range(heads_here):
        attended = (acc_ref[head] / sum_ref[head]).astype(jnp.bfloat16)
        att_ref[:, :, head * HD : (head + 1) * HD] = attended.reshape(n, rows, HD)

    @pl.when(ends)
    def _():
        att_copy().start()

    load_out.wait()

    @pl.when(helper)
    def _():
        for by in range(chips):
            from_partner(by).wait_recv()
        att_copy().wait_recv()

    cols = width // halves

    def sum_copy(way, step, piece):
        side = (way + 1) // 2
        span = pl.ds(piece * cols, cols)
        return pltpu.make_async_remote_copy(
            src_ref=going.at[side, step].at[:, span],
            dst_ref=landed.at[side, step].at[:, span],
            send_sem=s_send.at[side, step, piece],
            recv_sem=s_recv.at[side, step, piece],
            device_id={"head": me + way},
            device_id_type=MESH,
        )

    def product(block, piece):
        return jnp.dot(
            att_ref[block],
            w_ref[:, piece * cols : (piece + 1) * cols],
            preferred_element_type=jnp.float32,
        )

    def far_product(block, piece):
        return jnp.dot(
            att_far[block],
            w_far[:, piece * cols : (piece + 1) * cols],
            preferred_element_type=jnp.float32,
        )

    def helps(way):
        return me == (1 if way == 1 else n - 2)

    def owner(way, step):
        return (n - 1 - step) if way == 1 else step

    def sum_sends(way, step):
        block = owner(way, step)
        return (block > me) & (me > 0) if way == 1 else (block < me) & (me < n - 1)

    def sum_receives(way, step):
        block = owner(way, step)
        return (block >= me) & (me > 1) if way == 1 else (block <= me) & (me < n - 2)

    @pl.loop(0, n - 1)
    def _(tick):
        for piece in range(halves):
            span = slice(piece * cols, (piece + 1) * cols)
            for way in (-1, 1):
                side = (way + 1) // 2
                step = tick - (me if way == 1 else n - 1 - me)
                held = (step >= 0) & (step < n - 1)

                @pl.when(held & sum_sends(way, step))
                def _():
                    going[side, step, :, span] = product(owner(way, step), piece).astype(
                        going.dtype
                    )

                    @pl.when(helps(way))
                    def _():
                        going[side, step, :, span] = (
                            going[side, step, :, span].astype(jnp.float32)
                            + far_product(owner(way, step), piece)
                        ).astype(going.dtype)

                    @pl.when(sum_receives(way, step))
                    def _():
                        sum_copy(way, step, piece).wait_recv()
                        going[side, step, :, span] = (
                            going[side, step, :, span].astype(jnp.float32)
                            + landed[side, step, :, span].astype(jnp.float32)
                        ).astype(going.dtype)

                    sum_copy(way, step, piece).start()

    for piece in range(halves):
        span = slice(piece * cols, (piece + 1) * cols)
        total_ref[:, span] = product(me, piece).astype(going.dtype).astype(jnp.float32)
    for piece in range(halves):
        span = slice(piece * cols, (piece + 1) * cols)
        for way in (-1, 1):
            side = (way + 1) // 2
            last = n - 1 - me if way == 1 else me

            @pl.when(helps(way))
            def _():
                total_ref[:, span] += far_product(me, piece)

            @pl.when(me > 1 if way == 1 else me < n - 2)
            def _():
                sum_copy(way, last, piece).wait_recv()
                total_ref[:, span] += landed[side, last, :, span].astype(jnp.float32)

        out_ref[0, :, span] = (
            total_ref[:, span] * table_ref[2, pl.ds(level, 1), span]
        ).astype(out_ref.dtype)

    @pl.loop(0, n - 1)
    def _(step):
        for piece in range(halves):
            for way in (-1, 1):

                @pl.when(sum_sends(way, step))
                def _():
                    sum_copy(way, step, piece).wait_send()

    @pl.loop(0, n)
    def _(block):
        for ahead in range(1, tracts):

            @pl.when(tract + ahead < tracts)
            def _():
                kv_copy(ahead, block).wait_send()

    @pl.loop(0, n - 1)
    def _(step):
        for piece in range(pieces):
            for way in (-1, 1):

                @pl.when(sends(way, step))
                def _():
                    copy(way, step, piece).wait_send()

    @pl.when(ends)
    def _():
        to_helper().wait_send()
        att_copy().wait_send()

    @pl.when(helper)
    def _():
        for by in range(1, chips):
            to_chip(by).wait_send()
        for by in range(chips):
            to_partner(by).wait_send()


def ring_body(frames, levels, visible, w_qkv, w_out, modulation):
    n, tracts = lax.axis_size("head"), lax.axis_size("tract")
    reps = lax.axis_size("rep")
    rows, width = frames.shape[1:]
    cols = w_qkv.shape[2]
    heads_here = cols // HD
    pieces = max(1, rows // 32)
    halves = 4 if width % 512 == 0 else 2
    vmem = pl.BlockSpec(memory_space=pltpu.VMEM)
    hbm = pl.BlockSpec(memory_space=pltpu.HBM)
    smem = pl.BlockSpec(memory_space=pltpu.SMEM)
    half = jnp.bfloat16
    dma = pltpu.SemaphoreType.DMA
    return pl.pallas_call(
        functools.partial(sublayer_kernel, n, tracts, reps, pieces, halves),
        out_shape=jax.ShapeDtypeStruct(frames.shape, frames.dtype),
        in_specs=[hbm, smem, smem, hbm, hbm, vmem],
        out_specs=vmem,
        scratch_shapes=[
            pltpu.VMEM((n, rows, width), half),
            pltpu.VMEM((3, width, cols), half),
            pltpu.VMEM(w_out.shape, half),
            pltpu.VMEM((n, rows, cols), half),
            pltpu.VMEM((n, 2, rows, cols), half),
            pltpu.VMEM((max(1, tracts - 1), n, 2, rows, cols), half),
            pltpu.VMEM((n, rows, cols), half),
            pltpu.VMEM((heads_here, n * rows, 1), jnp.float32),
            pltpu.VMEM((heads_here, n * rows, 1), jnp.float32),
            pltpu.VMEM((heads_here, n * rows, HD), jnp.float32),
            pltpu.VMEM((2, n - 1, rows, width), half),
            pltpu.VMEM((2, n - 1, rows, width), half),
            pltpu.VMEM((rows, width), jnp.float32),
            dma((3,)),
            dma((2, n, pieces)),
            dma((2, n, pieces)),
            dma((tracts, n)),
            dma((tracts, n)),
            dma((2, n, halves)),
            dma((2, n, halves)),
            pltpu.VMEM(w_out.shape, half),
            pltpu.VMEM((n, rows, cols), half),
            dma((tracts * reps + 1,)),
            dma((tracts * reps + 1,)),
        ],
        compiler_params=pltpu.CompilerParams(
            collective_id=0, has_side_effects=True, vmem_limit_bytes=GRANT
        ),
    )(
        frames,
        levels,
        visible,
        jnp.transpose(w_qkv, (1, 0, 2)),
        w_out,
        jnp.transpose(modulation, (1, 0, 2)),
    )


def line_kernel(
    n,
    tracts,
    reps,
    pieces,
    near,
    x_ref,
    level_ref,
    visible_ref,
    w_hbm,
    out_hbm,
    table_ref,
    out_ref,
    raw,
    got,
    wq_ref,
    w_far,
    wo_ref,
    acc_ref,
    q_ref,
    kv_ref,
    kv_in,
    part_ref,
    part_in,
    att_ref,
    peak_ref,
    sum_ref,
    mix_ref,
    att_all,
    out_part,
    out_in,
    load_sem,
    wq_sem,
    g_send,
    g_recv,
    f_send,
    f_recv,
    p_send,
    p_recv,
    kv_send,
    kv_recv,
    wo_send,
    wo_recv,
    z_send,
    z_recv,
    a_send,
    a_recv,
    o_send,
    o_recv,
):
    me, tract, rep = lax.axis_index("head"), lax.axis_index("tract"), lax.axis_index("rep")
    rows, width = x_ref.shape[1:]
    deep = width // pieces
    low = me < 2
    sign = jnp.where(low, 1, -1)
    base = jnp.where(low, 0, n - 1)
    is_end = (me == 0) | (me == n - 1)
    is_helper = (me == 1) | (me == n - 2)
    inner, outer = {"head": me + sign}, {"head": me - sign}

    def blk(r):
        return base + sign * r

    core, wide = tract % 2, tracts // 2
    chips = wide * reps
    seats = chips * 2
    chip = rep * wide + tract // 2
    seat = chip * 2 + core
    partner = {"tract": tract + 1 - 2 * core}

    def chip_at(by):
        return lax.rem(chip + by, chips)

    def place(which, side):
        return {"rep": which // wide, "tract": lax.rem(which, wide) * 2 + side}

    own_load = pltpu.make_async_copy(x_ref.at[0], raw, load_sem.at[0])
    own_load.start()
    cols_out = width // seats
    out_span = pl.ds(pl.multiple_of(seat * cols_out, 128), cols_out)
    wo_load = pltpu.make_async_copy(out_hbm.at[:, out_span], wo_ref.at[me], load_sem.at[1])

    def wq_load(p):
        span = pl.ds(pl.multiple_of(p * deep, deep), deep)
        return pltpu.make_async_copy(w_hbm.at[:, span], wq_ref.at[:, span], wq_sem.at[p])

    @pl.loop(0, pieces)
    def _(p):
        wq_load(p).start()

    wo_load.start()

    barrier = pltpu.get_barrier_semaphore()
    for ahead in range(1, n):
        other = lax.rem(me + ahead, n)
        pl.semaphore_signal(barrier, inc=1, device_id={"head": other}, device_id_type=MESH)
    for by in range(chips):
        for side in range(2):
            if by == 0 and side == 1:
                continue
            target = partner if by == 0 else place(chip_at(by), side)
            pl.semaphore_signal(barrier, inc=1, device_id=target, device_id_type=MESH)

    level = level_ref[0]

    def style(kind, start):
        return table_ref[kind, pl.ds(level, 1), start : start + deep]

    def remote(src, dst, send, recv, target):
        return pltpu.make_async_remote_copy(
            src_ref=src,
            dst_ref=dst,
            send_sem=send,
            recv_sem=recv,
            device_id=target,
            device_id_type=MESH,
        )

    def tok(way, r, p):
        b = blk(r)
        ref = got.at[b, p]
        target = inner if way == 0 else outer
        return remote(ref, ref, g_send.at[way, b, p], g_recv.at[b, p], target)

    far_rows = w_far.shape[1] // seats
    far_base = near * deep

    def far_span(which, side):
        start = (which * 2 + side) * far_rows
        return pl.ds(pl.multiple_of(start, far_rows), far_rows)

    def far_first(kind):
        start = far_base + seat * far_rows
        src = w_hbm.at[kind, pl.ds(pl.multiple_of(start, far_rows), far_rows)]
        dst = w_far.at[kind, far_span(chip, core)]
        return remote(src, dst, f_send.at[0, kind], f_recv.at[0, kind], inner)

    def far_chip(by, kind, which):
        ref = w_far.at[kind, far_span(which, core)]
        return remote(ref, ref, f_send.at[by, kind], f_recv.at[by, kind], place(chip_at(by), core))

    def far_out(by, kind):
        return far_chip(by, kind, chip)

    def far_in(by, kind):
        return far_chip(by, kind, chip_at(chips - by))

    def far_pass(by, kind, side):
        ref = w_far.at[kind, far_span(chip_at(chips - by), side)]
        where = chips + by
        return remote(ref, ref, f_send.at[where, kind], f_recv.at[where, kind], partner)

    def far_relay(kind):
        far_first(kind).wait_recv()
        for by in range(1, chips):
            far_out(by, kind).start()
        far_pass(0, kind, core).start()

    def far_hand(kind):
        for by in range(1, chips):
            far_in(by, kind).wait_recv()
            far_pass(by, kind, core).start()

    def far_ready(kind):
        for by in range(chips):
            far_pass(by, kind, 1 - core).wait_recv()

    def part_copy(r, kind):
        b = blk(r)
        return remote(
            part_ref.at[b, kind],
            part_in.at[b, kind],
            p_send.at[b, kind],
            p_recv.at[b, kind],
            outer,
        )

    def far_part(rs, kinds):
        for kind in kinds:
            total = None
            for p in range(near, pieces):
                lhs = jnp.concatenate([got[blk(r), p] for r in rs], axis=0)
                span = slice((p - near) * deep, (p - near + 1) * deep)
                made = jnp.dot(lhs, w_far[kind, span], preferred_element_type=jnp.float32)
                total = made if total is None else total + made
            total = total.astype(part_ref.dtype)
            for i, r in enumerate(rs):
                part_ref[blk(r), kind] = total[i * rows : (i + 1) * rows]
        for r in rs:
            for kind in kinds:
                part_copy(r, kind).start()

    cuts = wo_send.shape[2]
    wo_rows = wo_ref.shape[1] // cuts

    def wo_copy(way, r, cut):
        b = blk(r)
        ref = wo_ref.at[b, pl.ds(cut * wo_rows, wo_rows)]
        target = inner if way == 0 else outer
        return remote(ref, ref, wo_send.at[way, b, cut], wo_recv.at[b, cut], target)

    def wo_start(way, r):
        for cut in range(cuts):
            wo_copy(way, r, cut).start()

    def wo_forward(way, r):
        for cut in range(cuts):
            wo_copy(way, r, cut).wait_recv()
            wo_copy(way, r, cut).start()

    def kv_copy(ahead, block):
        return remote(
            kv_ref.at[block],
            kv_in.at[ahead - 1, block],
            kv_send.at[ahead - 1, block],
            kv_recv.at[ahead - 1, block],
            {"tract": tract + ahead},
        )

    def accumulate(rs, p):
        lhs = jnp.concatenate([got[blk(r), p] for r in rs], axis=0)
        span = pl.ds(pl.multiple_of(p * deep, deep), deep)
        for kind in range(3):
            made = jnp.dot(lhs, wq_ref[kind, span], preferred_element_type=jnp.float32)
            for i, r in enumerate(rs):
                acc_ref[blk(r), kind] += made[i * rows : (i + 1) * rows]

    def settle(r, kinds, extra=False):
        b = blk(r)
        for kind in kinds:
            made = acc_ref[b, kind]
            if extra:
                made = made + part_in[b, kind].astype(jnp.float32)
            made = made.astype(q_ref.dtype)
            if kind == 0:
                q_ref[b] = made
            else:
                kv_ref[b, kind - 1] = made

    def share(r):
        for ahead in range(1, tracts):

            @pl.when(tract + ahead < tracts)
            def _():
                kv_copy(ahead, blk(r)).start()

    acc_ref[...] = jnp.zeros_like(acc_ref)
    own_load.wait()
    power = jnp.zeros((rows, 1), jnp.float32)
    for p in range(pieces):
        tokens = raw[:, p * deep : (p + 1) * deep].astype(jnp.float32)
        power += jnp.sum(tokens * tokens, axis=-1, keepdims=True)
    factor = lax.rsqrt(power * (1.0 / width) + 1e-06)
    for p in range(pieces):
        tokens = raw[:, p * deep : (p + 1) * deep].astype(jnp.float32)
        shaped = tokens * factor * (1.0 + style(1, p * deep)) + style(0, p * deep)
        got[me, p] = shaped.astype(got.dtype)
    pl.semaphore_wait(barrier, n - 1 + seats - 1)

    @pl.when(is_end)
    def _():
        for kind in (1, 2, 0):
            far_first(kind).start()

        @pl.loop(0, pieces)
        def _(j):
            tok(0, 0, lax.rem(j + near, pieces)).start()

        wo_load.wait()
        wo_start(0, 0)

        @pl.loop(0, pieces)
        def _(p):
            wq_load(p).wait()
            accumulate((0,), p)

        settle(0, (1, 2, 0))
        share(0)
        for r in (1, 2):

            @pl.loop(0, near)
            def _(p):
                tok(0, r, p).wait_recv()
                accumulate((r,), p)

        for r in (1, 2):
            for kind in (1, 2):
                part_copy(r, kind).wait_recv()
            settle(r, (1, 2), True)
            share(r)

        @pl.loop(0, near)
        def _(p):
            tok(0, 3, p).wait_recv()
            accumulate((3,), p)

        for kind in (1, 2):
            part_copy(3, kind).wait_recv()
        settle(3, (1, 2), True)
        share(3)
        for r in (1, 2, 3):
            part_copy(r, 0).wait_recv()
            settle(r, (0,), True)

    @pl.when(is_helper)
    def _():
        @pl.loop(0, near)
        def _(p):
            tok(0, 1, p).start()
            tok(1, 1, p).start()

        @pl.loop(near, pieces)
        def _(p):
            tok(0, 1, p).start()

        wo_load.wait()

        @pl.loop(0, pieces)
        def _(p):
            wq_load(p).wait()
            tok(1, 2, p).wait_recv()

            @pl.when(p < near)
            def _():
                tok(1, 2, p).start()

            accumulate((1, 2), p)
            for at, kind in ((1, 1), (3, 2), (5, 0)):

                @pl.when(p == at)
                def _():
                    far_relay(kind)

            @pl.when(p == pieces - 2)
            def _():
                far_hand(1)

        settle(1, (1, 2, 0))
        share(1)
        settle(2, (1, 2, 0))
        share(2)
        wo_start(1, 1)
        far_ready(1)
        far_part((1, 2), (1,))

        @pl.loop(0, pieces)
        def _(j):
            p = lax.rem(j + near, pieces)
            tok(0, 0, p).wait_recv()
            tok(0, 0, p).start()
            tok(1, 3, p).wait_recv()

            @pl.when(p < near)
            def _():
                tok(1, 3, p).start()

            accumulate((0, 3), p)

            @pl.when(j == 2)
            def _():
                far_hand(2)

            @pl.when(j == 3)
            def _():
                far_ready(2)
                far_part((1, 2), (2,))

            @pl.when(j == 5)
            def _():
                far_hand(0)
                far_part((3,), (1, 2))
                far_ready(0)
                far_part((1, 2, 3), (0,))

        settle(0, (1, 2, 0))
        share(0)
        settle(3, (1, 2, 0))
        share(3)
        wo_start(0, 1)

    tokens_here = n * rows
    heads_here = q_ref.shape[2] // HD
    scale = HD ** (-0.5)

    def attend(source, allowed):
        for head in range(heads_here):
            lanes = slice(head * HD, (head + 1) * HD)
            queries = q_ref[:, :, lanes].reshape(tokens_here, HD)
            keys = source[:, 0, :, lanes].reshape(tokens_here, HD)
            values = source[:, 1, :, lanes].reshape(tokens_here, HD)
            scores = (
                lax.dot_general(
                    queries, keys, (((1,), (1,)), ((), ())), preferred_element_type=jnp.float32
                )
                * scale
            )
            if allowed is None:
                peak = jnp.max(scores, axis=1, keepdims=True)
                probs = jnp.exp(scores - peak)
            else:
                scores = jnp.where(allowed, scores, -1e30)
                old = peak_ref[head]
                peak = jnp.maximum(old, jnp.max(scores, axis=1, keepdims=True))
                probs = jnp.where(allowed, jnp.exp(scores - peak), 0.0)
                rescale = jnp.exp(old - peak)
            row_sum = jnp.sum(probs, axis=1, keepdims=True)
            weighted = jnp.dot(
                probs.astype(jnp.bfloat16), values, preferred_element_type=jnp.float32
            )
            if allowed is not None:
                row_sum += sum_ref[head] * rescale
                weighted += mix_ref[head] * rescale
            peak_ref[head] = peak
            sum_ref[head] = row_sum
            mix_ref[head] = weighted

    attend(kv_ref, None)

    @pl.when(is_helper)
    def _():
        wo_forward(0, 0)

    for ahead in range(1, tracts):

        @pl.when(tract >= ahead)
        def _():
            @pl.loop(0, n)
            def _(block):
                kv_copy(ahead, block).wait_recv()

            attend(kv_in.at[ahead - 1], visible_ref[0, lax.max(tract - ahead, 0)] > 0)

    for head in range(heads_here):
        attended = (mix_ref[head] / sum_ref[head]).astype(jnp.bfloat16)
        att_ref[:, :, head * HD : (head + 1) * HD] = attended.reshape(n, rows, HD)

    def att_line(other, source):
        return remote(
            att_ref.at[other],
            att_all.at[seat, source],
            z_send.at[other],
            z_recv.at[source],
            {"head": other},
        )

    for ahead in range(1, n):
        other = lax.rem(me + ahead, n)
        att_line(other, me).start()
    att_all[seat, me] = att_ref[me]

    @pl.when(is_helper)
    def _():
        wo_forward(1, 2)

    def att_chip(by, z, which):
        ref = att_all.at[which * 2 + core, z]
        return remote(ref, ref, a_send.at[by, z], a_recv.at[by, z], place(chip_at(by), core))

    def att_pass(by, z, side):
        ref = att_all.at[chip_at(chips - by) * 2 + side, z]
        where = chips + by
        return remote(ref, ref, a_send.at[where, z], a_recv.at[where, z], partner)

    for ahead in range(n):
        z = lax.rem(me + ahead, n)
        if ahead:
            att_line(z, z).wait_recv()
        for by in range(1, chips):
            att_chip(by, z, chip).start()
        att_pass(0, z, core).start()

    @pl.when(is_helper)
    def _():
        wo_forward(1, 3)

    for ahead in range(n):
        z = lax.rem(me + ahead, n)
        for by in range(1, chips):
            att_chip(by, z, chip_at(chips - by)).wait_recv()
            att_pass(by, z, core).start()

    @pl.when(is_end)
    def _():
        for r in (1, 2, 3):
            for cut in range(cuts):
                wo_copy(0, r, cut).wait_recv()

    def out_copy(which, side, source):
        return remote(
            out_part.at[which * 2 + side],
            out_in.at[source],
            o_send.at[which * 2 + side],
            o_recv.at[source],
            place(which, side),
        )

    heads_wide = wo_ref.shape[1]
    for step in range(1, chips + 1):
        by = step % chips
        which = chip_at(chips - by)
        for z in range(n):
            att_pass(by, z, 1 - core).wait_recv()
        total = None
        for z in range(n):
            lhs = att_all[pl.ds(which * 2, 2), z].reshape(2 * rows, heads_wide)
            made = jnp.dot(lhs, wo_ref[z], preferred_element_type=jnp.float32)
            total = made if total is None else total + made
        total = total.astype(out_part.dtype)
        for side in range(2):
            out_part[which * 2 + side] = total[side * rows : (side + 1) * rows]
        if by:
            for side in range(2):
                out_copy(which, side, seat).start()
        else:
            out_copy(chip, 1 - core, seat).start()

    def finish(ref, source):
        span = pl.ds(pl.multiple_of(source * cols_out, 128), cols_out)
        gate = table_ref[2, pl.ds(level, 1), span]
        out_ref[0, :, span] = (ref[source].astype(jnp.float32) * gate).astype(out_ref.dtype)

    finish(out_part, seat)
    for by in range(chips):
        for side in range(2):
            if by == 0 and side == 0:
                continue
            lane = core if side == 0 else 1 - core
            source = chip_at(chips - by) * 2 + lane
            out_copy(chip, core, source).wait_recv()
            finish(out_in, source)

    for by in range(chips):
        for side in range(2):
            if by == 0 and side == 0:
                continue
            lane = core if side == 0 else 1 - core
            out_copy(chip_at(chips - by), lane, seat).wait_send()
    for z in range(n):
        for by in range(1, chips):
            att_chip(by, z, chip).wait_send()
        for by in range(chips):
            att_pass(by, z, core).wait_send()
    for ahead in range(1, n):
        att_line(lax.rem(me + ahead, n), me).wait_send()

    @pl.loop(0, n)
    def _(block):
        for ahead in range(1, tracts):

            @pl.when(tract + ahead < tracts)
            def _():
                kv_copy(ahead, block).wait_send()

    @pl.when(is_end)
    def _():
        for kind in range(3):
            far_first(kind).wait_send()

        @pl.loop(0, pieces)
        def _(p):
            tok(0, 0, p).wait_send()

        for cut in range(cuts):
            wo_copy(0, 0, cut).wait_send()

    @pl.when(is_helper)
    def _():
        for kind in range(3):
            for by in range(1, chips):
                far_out(by, kind).wait_send()
            for by in range(chips):
                far_pass(by, kind, core).wait_send()
            for r in (1, 2, 3):
                part_copy(r, kind).wait_send()

        @pl.loop(0, pieces)
        def _(p):
            for r in (0, 1):
                tok(0, r, p).wait_send()

        @pl.loop(0, near)
        def _(p):
            for r in (1, 2, 3):
                tok(1, r, p).wait_send()

        for cut in range(cuts):
            for r in (0, 1):
                wo_copy(0, r, cut).wait_send()
            for r in (1, 2, 3):
                wo_copy(1, r, cut).wait_send()


PIECES = 8
NEAR = 4


def fits_line(n, tracts, reps, frames, w_out):
    rows, width = frames.shape[1:]
    seats = tracts * reps
    far = (PIECES - NEAR) * (width // PIECES)
    return (
        n == 4
        and tracts % 2 == 0
        and seats > 2
        and rows % 16 == 0
        and width % (PIECES * 128) == 0
        and width % (seats * 128) == 0
        and far % (seats * 16) == 0
        and w_out.shape[0] % 32 == 0
    )


def line_body(frames, levels, visible, w_qkv, w_out, modulation):
    n, tracts = lax.axis_size("head"), lax.axis_size("tract")
    reps = lax.axis_size("rep")
    rows, width = frames.shape[1:]
    cols = w_qkv.shape[2]
    heads_here = cols // HD
    seats = tracts * reps
    chips = seats // 2
    deep = width // PIECES
    vmem = pl.BlockSpec(memory_space=pltpu.VMEM)
    hbm = pl.BlockSpec(memory_space=pltpu.HBM)
    smem = pl.BlockSpec(memory_space=pltpu.SMEM)
    half = jnp.bfloat16
    dma = pltpu.SemaphoreType.DMA
    return pl.pallas_call(
        functools.partial(line_kernel, n, tracts, reps, PIECES, NEAR),
        out_shape=jax.ShapeDtypeStruct(frames.shape, frames.dtype),
        in_specs=[hbm, smem, smem, hbm, hbm, vmem],
        out_specs=vmem,
        scratch_shapes=[
            pltpu.VMEM((rows, width), half),
            pltpu.VMEM((n, PIECES, rows, deep), half),
            pltpu.VMEM((3, width, cols), half),
            pltpu.VMEM((3, (PIECES - NEAR) * deep, cols), half),
            pltpu.VMEM((n, w_out.shape[0], width // seats), half),
            pltpu.VMEM((n, 3, rows, cols), jnp.float32),
            pltpu.VMEM((n, rows, cols), half),
            pltpu.VMEM((n, 2, rows, cols), half),
            pltpu.VMEM((max(1, tracts - 1), n, 2, rows, cols), half),
            pltpu.VMEM((n, 3, rows, cols), half),
            pltpu.VMEM((n, 3, rows, cols), half),
            pltpu.VMEM((n, rows, cols), half),
            pltpu.VMEM((heads_here, n * rows, 1), jnp.float32),
            pltpu.VMEM((heads_here, n * rows, 1), jnp.float32),
            pltpu.VMEM((heads_here, n * rows, HD), jnp.float32),
            pltpu.VMEM((seats, n, rows, cols), half),
            pltpu.VMEM((seats, rows, width // seats), half),
            pltpu.VMEM((seats, rows, width // seats), half),
            dma((2,)),
            dma((PIECES,)),
            dma((2, n, PIECES)),
            dma((n, PIECES)),
            dma((2 * chips, 3)),
            dma((2 * chips, 3)),
            dma((n, 3)),
            dma((n, 3)),
            dma((tracts, n)),
            dma((tracts, n)),
            dma((2, n, 2)),
            dma((n, 2)),
            dma((n,)),
            dma((n,)),
            dma((2 * chips, n)),
            dma((2 * chips, n)),
            dma((seats,)),
            dma((seats,)),
        ],
        compiler_params=pltpu.CompilerParams(
            collective_id=0, has_side_effects=True, vmem_limit_bytes=GRANT
        ),
    )(
        frames,
        levels,
        visible,
        jnp.transpose(w_qkv, (1, 0, 2)),
        w_out,
        jnp.transpose(modulation, (1, 0, 2)),
    )


def body(frames, levels, visible, w_qkv, w_out, modulation):
    n, tracts = lax.axis_size("head"), lax.axis_size("tract")
    reps = lax.axis_size("rep")
    line = fits_line(n, tracts, reps, frames, w_out)
    chosen = line_body if line else ring_body
    return chosen(frames, levels, visible, w_qkv, w_out, modulation)


def solution(mesh):
    placed = (
        P(("rep", "tract"), "head", None),
        P(("rep", "tract")),
        P(("rep", "tract"), None),
        P(None, None, "head"),
        P("head", None),
        P(),
    )
    return jax.shard_map(
        body,
        mesh=mesh,
        in_specs=placed,
        out_specs=P(("rep", "tract"), "head", None),
        check_vma=False,
    )
```

profile of v0, /device:TPU:0, one launch (start us, length us, event | category | flops | bytes accessed | tf_op | source)
XLA Modules:
  0.0 109.6 jit_solution(17411076878251148558)
XLA Ops:
  0.7 106.9 %shard_map.64 = bf16[1,64,6144]{2,1,0:T(8,128)(2,1)} custom-call(bf16[1,64,6144]{2,1,0:T(8,128)(2,1)} %x_ref.1, s32[1]{0:T(128)S(6)} %copy.8.level_ref, s32[1,4]{1,0:T(1,128)} %visible_ref.1, bf16[3,6144,256]{2,1,0:T(8,128)(2,1)} %bitcast.2, bf16[256,6144]{1,0:T(8,128)(2,1)} %out_hbm.1, f32[3,8,6144]{2,1,0:T(8,128)} %bitcast.3), custom_call_target="tpu_custom_call" | custom-call | tf_op jit(solution)/shard_map/pallas_call | solution.py:1129
  107.5 2.1 %copy.9 = bf16[1,64,6144]{2,1,0:T(8,128)(2,1)} copy(bf16[1,64,6144]{2,1,0:T(8,128)(2,1)} %shard_map.64) | data formatting | bytes 1572864
where the time goes:
time: 110 us
  Pallas kernels  107 us (97%)
  local copies, waits for them, and re-layouts  2.06 us (2%)
    pallas_call x1, Pallas kernels, line_body(): pl.pallas_call(functools.partial(line_kernel, n, tracts, reps, PIECES, NE...  107 us

commit v1 on v0

--- a/solution.py
+++ b/solution.py
@@ -511,8 +511,9 @@
     visible_ref,
     w_hbm,
     out_hbm,
+    table_hbm,
+    out_ref,
     table_ref,
-    out_ref,
     raw,
     got,
     wq_ref,
@@ -533,6 +534,7 @@
     out_in,
     load_sem,
     wq_sem,
+    wo_sem,
     g_send,
     g_recv,
     f_send,
@@ -578,9 +580,17 @@
 
     own_load = pltpu.make_async_copy(x_ref.at[0], raw, load_sem.at[0])
     own_load.start()
+    table_load = pltpu.make_async_copy(table_hbm, table_ref, load_sem.at[1])
+    table_load.start()
     cols_out = width // seats
-    out_span = pl.ds(pl.multiple_of(seat * cols_out, 128), cols_out)
-    wo_load = pltpu.make_async_copy(out_hbm.at[:, out_span], wo_ref.at[me], load_sem.at[1])
+    cuts = wo_ref.shape[1]
+    cut_cols = cols_out // cuts
+
+    def wo_load(cut):
+        start = pl.multiple_of(seat * cols_out + cut * cut_cols, 128)
+        src = out_hbm.at[:, pl.ds(start, cut_cols)]
+        return pltpu.make_async_copy(src, wo_ref.at[me, cut], wo_sem.at[cut])
+
 
     def wq_load(p):
         span = pl.ds(pl.multiple_of(p * deep, deep), deep)
@@ -590,7 +600,8 @@
     def _(p):
         wq_load(p).start()
 
-    wo_load.start()
+    for cut in range(cuts):
+        wo_load(cut).start()
 
     barrier = pltpu.get_barrier_semaphore()
     for ahead in range(1, n):
@@ -692,23 +703,19 @@
             for kind in kinds:
                 part_copy(r, kind).start()
 
-    cuts = wo_send.shape[2]
-    wo_rows = wo_ref.shape[1] // cuts
-
     def wo_copy(way, r, cut):
         b = blk(r)
-        ref = wo_ref.at[b, pl.ds(cut * wo_rows, wo_rows)]
+        ref = wo_ref.at[b, cut]
         target = inner if way == 0 else outer
         return remote(ref, ref, wo_send.at[way, b, cut], wo_recv.at[b, cut], target)
 
-    def wo_start(way, r):
-        for cut in range(cuts):
+    def wo_start(way, r, which):
+        for cut in which:
             wo_copy(way, r, cut).start()
 
-    def wo_forward(way, r):
-        for cut in range(cuts):
-            wo_copy(way, r, cut).wait_recv()
-            wo_copy(way, r, cut).start()
+    def wo_forward(way, r, cut):
+        wo_copy(way, r, cut).wait_recv()
+        wo_copy(way, r, cut).start()
 
     def kv_copy(ahead, block):
         return remote(
@@ -752,6 +759,7 @@
     for p in range(pieces):
         tokens = raw[:, p * deep : (p + 1) * deep].astype(jnp.float32)
         power += jnp.sum(tokens * tokens, axis=-1, keepdims=True)
+    table_load.wait()
     factor = lax.rsqrt(power * (1.0 / width) + 1e-06)
     for p in range(pieces):
         tokens = raw[:, p * deep : (p + 1) * deep].astype(jnp.float32)
@@ -768,13 +776,14 @@
         def _(j):
             tok(0, 0, lax.rem(j + near, pieces)).start()
 
-        wo_load.wait()
-        wo_start(0, 0)
-
         @pl.loop(0, pieces)
         def _(p):
             wq_load(p).wait()
             accumulate((0,), p)
+
+        for cut in range(cuts):
+            wo_load(cut).wait()
+        wo_start(0, 0, range(cuts))
 
         settle(0, (1, 2, 0))
         share(0)
@@ -815,8 +824,6 @@
         def _(p):
             tok(0, 1, p).start()
 
-        wo_load.wait()
-
         @pl.loop(0, pieces)
         def _(p):
             wq_load(p).wait()
@@ -841,15 +848,28 @@
         share(1)
         settle(2, (1, 2, 0))
         share(2)
-        wo_start(1, 1)
+        for cut in range(cuts):
+            wo_load(cut).wait()
+        wo_start(1, 1, range(cuts))
         far_ready(1)
         far_part((1, 2), (1,))
 
-        @pl.loop(0, pieces)
-        def _(j):
+        def pass_on(j):
             p = lax.rem(j + near, pieces)
             tok(0, 0, p).wait_recv()
             tok(0, 0, p).start()
+
+        @pl.loop(0, 2)
+        def _(j):
+            pass_on(j)
+
+        @pl.loop(0, pieces)
+        def _(j):
+            @pl.when(j + 2 < pieces)
+            def _():
+                pass_on(j + 2)
+
+            p = lax.rem(j + near, pieces)
             tok(1, 3, p).wait_recv()
 
             @pl.when(p < near)
@@ -878,7 +898,9 @@
         share(0)
         settle(3, (1, 2, 0))
         share(3)
-        wo_start(0, 1)
+        for cut in range(cuts - 1):
+            wo_start(0, 1, (cut,))
+            wo_forward(0, 0, cut)
 
     tokens_here = n * rows
     heads_here = q_ref.shape[2] // HD
@@ -918,10 +940,6 @@
 
     attend(kv_ref, None)
 
-    @pl.when(is_helper)
-    def _():
-        wo_forward(0, 0)
-
     for ahead in range(1, tracts):
 
         @pl.when(tract >= ahead)
@@ -952,7 +970,11 @@
 
     @pl.when(is_helper)
     def _():
-        wo_forward(1, 2)
+        wo_start(0, 1, (cuts - 1,))
+        wo_forward(0, 0, cuts - 1)
+        for cut in range(cuts - 1):
+            for r in (2, 3):
+                wo_forward(1, r, cut)
 
     def att_chip(by, z, which):
         ref = att_all.at[which * 2 + core, z]
@@ -973,7 +995,8 @@
 
     @pl.when(is_helper)
     def _():
-        wo_forward(1, 3)
+        for r in (2, 3):
+            wo_forward(1, r, cuts - 1)
 
     for ahead in range(n):
         z = lax.rem(me + ahead, n)
@@ -981,62 +1004,55 @@
             att_chip(by, z, chip_at(chips - by)).wait_recv()
             att_pass(by, z, core).start()
 
-    @pl.when(is_end)
-    def _():
-        for r in (1, 2, 3):
-            for cut in range(cuts):
-                wo_copy(0, r, cut).wait_recv()
-
-    def out_copy(which, side, source):
+    for z in range(n):
+        for by in range(chips):
+            att_pass(by, z, 1 - core).wait_recv()
+
+    def out_copy(which, side, source, cut):
         return remote(
-            out_part.at[which * 2 + side],
-            out_in.at[source],
-            o_send.at[which * 2 + side],
-            o_recv.at[source],
+            out_part.at[which * 2 + side, cut],
+            out_in.at[source, cut],
+            o_send.at[which * 2 + side, cut],
+            o_recv.at[source, cut],
             place(which, side),
         )
 
-    heads_wide = wo_ref.shape[1]
-    for step in range(1, chips + 1):
-        by = step % chips
-        which = chip_at(chips - by)
-        for z in range(n):
-            att_pass(by, z, 1 - core).wait_recv()
+    others = [(by, side) for by in range(1, chips) for side in range(2)] + [(0, 1)]
+    heads_wide = wo_ref.shape[2]
+    for cut in range(cuts):
+
+        @pl.when(is_end)
+        def _():
+            for r in (1, 2, 3):
+                wo_copy(0, r, cut).wait_recv()
+
         total = None
         for z in range(n):
-            lhs = att_all[pl.ds(which * 2, 2), z].reshape(2 * rows, heads_wide)
-            made = jnp.dot(lhs, wo_ref[z], preferred_element_type=jnp.float32)
+            lhs = att_all[:, z].reshape(seats * rows, heads_wide)
+            made = jnp.dot(lhs, wo_ref[z, cut], preferred_element_type=jnp.float32)
             total = made if total is None else total + made
-        total = total.astype(out_part.dtype)
-        for side in range(2):
-            out_part[which * 2 + side] = total[side * rows : (side + 1) * rows]
-        if by:
-            for side in range(2):
-                out_copy(which, side, seat).start()
-        else:
-            out_copy(chip, 1 - core, seat).start()
-
-    def finish(ref, source):
-        span = pl.ds(pl.multiple_of(source * cols_out, 128), cols_out)
+        out_part[:, cut] = total.astype(out_part.dtype).reshape(seats, rows, cut_cols)
+        for by, side in others:
+            lane = core if side == 0 else 1 - core
+            out_copy(chip_at(by), lane, seat, cut).start()
+
+    def finish(ref, source, cut):
+        span = pl.ds(pl.multiple_of(source * cols_out + cut * cut_cols, 128), cut_cols)
         gate = table_ref[2, pl.ds(level, 1), span]
-        out_ref[0, :, span] = (ref[source].astype(jnp.float32) * gate).astype(out_ref.dtype)
-
-    finish(out_part, seat)
-    for by in range(chips):
-        for side in range(2):
-            if by == 0 and side == 0:
-                continue
+        out_ref[0, :, span] = (ref[source, cut].astype(jnp.float32) * gate).astype(out_ref.dtype)
+
+    for cut in range(cuts):
+        finish(out_part, seat, cut)
+        for by, side in others:
             lane = core if side == 0 else 1 - core
             source = chip_at(chips - by) * 2 + lane
-            out_copy(chip, core, source).wait_recv()
-            finish(out_in, source)
-
-    for by in range(chips):
-        for side in range(2):
-            if by == 0 and side == 0:
-                continue
+            out_copy(chip, core, source, cut).wait_recv()
+            finish(out_in, source, cut)
+
+    for cut in range(cuts):
+        for by, side in others:
             lane = core if side == 0 else 1 - core
-            out_copy(chip_at(chips - by), lane, seat).wait_send()
+            out_copy(chip_at(by), lane, seat, cut).wait_send()
     for z in range(n):
         for by in range(1, chips):
             att_chip(by, z, chip).wait_send()
@@ -1106,7 +1122,7 @@
         and seats > 2
         and rows % 16 == 0
         and width % (PIECES * 128) == 0
-        and width % (seats * 128) == 0
+        and width % (seats * 256) == 0
         and far % (seats * 16) == 0
         and w_out.shape[0] % 32 == 0
     )
@@ -1121,6 +1137,7 @@
     seats = tracts * reps
     chips = seats // 2
     deep = width // PIECES
+    cuts = width // seats // 256
     vmem = pl.BlockSpec(memory_space=pltpu.VMEM)
     hbm = pl.BlockSpec(memory_space=pltpu.HBM)
     smem = pl.BlockSpec(memory_space=pltpu.SMEM)
@@ -1128,15 +1145,16 @@
     dma = pltpu.SemaphoreType.DMA
     return pl.pallas_call(
         functools.partial(line_kernel, n, tracts, reps, PIECES, NEAR),
-        out_shape=jax.ShapeDtypeStruct(frames.shape, frames.dtype),
-        in_specs=[hbm, smem, smem, hbm, hbm, vmem],
+        out_shape=pltpu.VMEM(frames.shape, frames.dtype),
+        in_specs=[hbm, smem, smem, hbm, hbm, hbm],
         out_specs=vmem,
         scratch_shapes=[
+            pltpu.VMEM((3, *modulation.shape[::2]), jnp.float32),
             pltpu.VMEM((rows, width), half),
             pltpu.VMEM((n, PIECES, rows, deep), half),
             pltpu.VMEM((3, width, cols), half),
             pltpu.VMEM((3, (PIECES - NEAR) * deep, cols), half),
-            pltpu.VMEM((n, w_out.shape[0], width // seats), half),
+            pltpu.VMEM((n, cuts, w_out.shape[0], 256), half),
             pltpu.VMEM((n, 3, rows, cols), jnp.float32),
             pltpu.VMEM((n, rows, cols), half),
             pltpu.VMEM((n, 2, rows, cols), half),
@@ -1148,10 +1166,11 @@
             pltpu.VMEM((heads_here, n * rows, 1), jnp.float32),
             pltpu.VMEM((heads_here, n * rows, HD), jnp.float32),
             pltpu.VMEM((seats, n, rows, cols), half),
-            pltpu.VMEM((seats, rows, width // seats), half),
-            pltpu.VMEM((seats, rows, width // seats), half),
+            pltpu.VMEM((seats, cuts, rows, 256), half),
+            pltpu.VMEM((seats, cuts, rows, 256), half),
             dma((2,)),
             dma((PIECES,)),
+            dma((cuts,)),
             dma((2, n, PIECES)),
             dma((n, PIECES)),
             dma((2 * chips, 3)),
@@ -1160,14 +1179,14 @@
             dma((n, 3)),
             dma((tracts, n)),
             dma((tracts, n)),
-            dma((2, n, 2)),
-            dma((n, 2)),
+            dma((2, n, cuts)),
+            dma((n, cuts)),
             dma((n,)),
             dma((n,)),
             dma((2 * chips, n)),
             dma((2 * chips, n)),
-            dma((seats,)),
-            dma((seats,)),
+            dma((seats, cuts)),
+            dma((seats, cuts)),
         ],
         compiler_params=pltpu.CompilerParams(
             collective_id=0, has_side_effects=True, vmem_limit_bytes=GRANT

time: 110 us -> 85.6 us (0.78)
  Pallas kernels: 107 us -> 83.9 us
  local copies, waits for them, and re-layouts: 2.06 us -> 0.88 us
    pallas_call x1, Pallas kernels: 107 us -> 83.9 us  [line_body(): pl.pallas_call(functools.partial(line_kernel, n, tracts, reps, PIECES, NE...]
    unnamed x1, local copies, waits for them, and re-layouts: 2.06 us -> 0.88 us
where the time goes in v1:
time: 85.6 us; the launch traced here: 85.4 us
  Pallas kernels  83.9 us (98%)
  local copies, waits for them, and re-layouts  0.88 us (1%)
    pallas_call x1, Pallas kernels, line_body(): pl.pallas_call(functools.partial(line_kernel, n, tracts, reps, PIECES, NE...  83.9 us

profile of v1, /device:TPU:0, one launch (start us, length us, event | category | flops | bytes accessed | tf_op | source)
XLA Modules:
  0.0 85.4 jit_solution(8355154502977702097)
XLA Ops:
  0.7 83.9 %shard_map.64 = bf16[1,64,6144]{2,1,0:T(8,128)(2,1)S(1)} custom-call(bf16[1,64,6144]{2,1,0:T(8,128)(2,1)} %x_ref.1, s32[1]{0:T(128)S(6)} %copy.9.level_ref, s32[1,4]{1,0:T(1,128)} %visible_ref.1, bf16[3,6144,256]{2,1,0:T(8,128)(2,1)} %bitcast.2, bf16[256,6144]{1,0:T(8,128)(2,1)} %out_hbm.1, f32[3,8,6144]{2,1,0:T(8,128)} %bitcast.3), custom_call_target="tpu_custom_call" | custom-call | tf_op jit(solution)/shard_map/pallas_call | solution.py:1146
  84.5 0.9 %copy.8 = bf16[1,64,6144]{2,1,0:T(8,128)(2,1)} copy(bf16[1,64,6144]{2,1,0:T(8,128)(2,1)S(1)} %shard_map.64) | data formatting | bytes 1572864

commit v2 on v1

--- a/solution.py
+++ b/solution.py
@@ -549,6 +549,7 @@
     z_recv,
     a_send,
     a_recv,
+    b_recv,
     o_send,
     o_recv,
 ):
@@ -633,7 +634,13 @@
         b = blk(r)
         ref = got.at[b, p]
         target = inner if way == 0 else outer
-        return remote(ref, ref, g_send.at[way, b, p], g_recv.at[b, p], target)
+        return remote(ref, ref, g_send.at[way, b], g_recv.at[b, p], target)
+
+    def tok_sent(way, r, count):
+        b = blk(r)
+        ref = got.at[b, pl.ds(0, count)]
+        target = inner if way == 0 else outer
+        remote(ref, ref, g_send.at[way, b], g_recv.at[b, 0], target).wait_send()
 
     far_rows = w_far.shape[1] // seats
     far_base = near * deep
@@ -646,44 +653,52 @@
         start = far_base + seat * far_rows
         src = w_hbm.at[kind, pl.ds(pl.multiple_of(start, far_rows), far_rows)]
         dst = w_far.at[kind, far_span(chip, core)]
-        return remote(src, dst, f_send.at[0, kind], f_recv.at[0, kind], inner)
-
-    def far_chip(by, kind, which):
+        return remote(src, dst, f_send.at[0], f_recv.at[0, kind], inner)
+
+    across = [
+        chip,
+        rep * wide + 1 - lax.rem(chip, wide),
+        (1 - rep) * wide + lax.rem(chip, wide),
+        (1 - rep) * wide + 1 - lax.rem(chip, wide),
+    ]
+    along_x, along_y = place(across[1], core), place(across[2], core)
+
+    def far_move(slot, kind, which):
         ref = w_far.at[kind, far_span(which, core)]
-        return remote(ref, ref, f_send.at[by, kind], f_recv.at[by, kind], place(chip_at(by), core))
-
-    def far_out(by, kind):
-        return far_chip(by, kind, chip)
-
-    def far_in(by, kind):
-        return far_chip(by, kind, chip_at(chips - by))
-
-    def far_pass(by, kind, side):
-        ref = w_far.at[kind, far_span(chip_at(chips - by), side)]
-        where = chips + by
-        return remote(ref, ref, f_send.at[where, kind], f_recv.at[where, kind], partner)
+        target = along_x if slot == 1 else along_y
+        return remote(ref, ref, f_send.at[slot], f_recv.at[slot, kind], target)
+
+    def far_pass(slot, kind, side):
+        ref = w_far.at[kind, far_span(across[slot], side)]
+        where = chips + slot
+        return remote(ref, ref, f_send.at[where], f_recv.at[where, kind], partner)
 
     def far_relay(kind):
         far_first(kind).wait_recv()
-        for by in range(1, chips):
-            far_out(by, kind).start()
+        far_move(1, kind, chip).start()
+        far_move(2, kind, chip).start()
         far_pass(0, kind, core).start()
 
-    def far_hand(kind):
-        for by in range(1, chips):
-            far_in(by, kind).wait_recv()
-            far_pass(by, kind, core).start()
+    def far_hand_x(kind):
+        far_move(1, kind, across[1]).wait_recv()
+        far_move(3, kind, across[1]).start()
+        far_pass(1, kind, core).start()
+
+    def far_hand_y(kind):
+        for slot in (2, 3):
+            far_move(slot, kind, across[slot]).wait_recv()
+            far_pass(slot, kind, core).start()
 
     def far_ready(kind):
-        for by in range(chips):
-            far_pass(by, kind, 1 - core).wait_recv()
+        for slot in range(chips):
+            far_pass(slot, kind, 1 - core).wait_recv()
 
     def part_copy(r, kind):
         b = blk(r)
         return remote(
             part_ref.at[b, kind],
             part_in.at[b, kind],
-            p_send.at[b, kind],
+            p_send.at[b],
             p_recv.at[b, kind],
             outer,
         )
@@ -707,24 +722,40 @@
         b = blk(r)
         ref = wo_ref.at[b, cut]
         target = inner if way == 0 else outer
-        return remote(ref, ref, wo_send.at[way, b, cut], wo_recv.at[b, cut], target)
+        return remote(ref, ref, wo_send.at[way, b], wo_recv.at[b, cut], target)
 
     def wo_start(way, r, which):
         for cut in which:
             wo_copy(way, r, cut).start()
 
+    along = [(0, r, cut) for cut in range(cuts) for r in (1, 0)]
+    back = [(1, r, cut) for cut in range(cuts) for r in (2, 3)]
+    early = 2
+
+    def wo_next(way, r, cut):
+        if r == 1:
+            wo_start(way, r, (cut,))
+        else:
+            wo_forward(way, r, cut)
+
     def wo_forward(way, r, cut):
         wo_copy(way, r, cut).wait_recv()
         wo_copy(way, r, cut).start()
 
-    def kv_copy(ahead, block):
-        return remote(
-            kv_ref.at[block],
-            kv_in.at[ahead - 1, block],
-            kv_send.at[ahead - 1, block],
-            kv_recv.at[ahead - 1, block],
-            {"tract": tract + ahead},
-        )
+    def kv_near(b):
+        ref, slot = kv_ref.at[b], kv_in.at[0, b]
+        return remote(ref, slot, kv_send.at[0], kv_recv.at[0], partner)
+
+    def kv_far(b):
+        ref, slot = kv_ref.at[b], kv_in.at[1, b]
+        return remote(ref, slot, kv_send.at[1], kv_recv.at[1], along_x)
+
+    def kv_relay():
+        slot = 2 * (1 - core)
+        return remote(kv_in.at[1], kv_in.at[slot], kv_send.at[2], kv_recv.at[slot], partner)
+
+    def kv_slot(slot):
+        return remote(kv_ref, kv_in.at[slot], kv_send.at[slot], kv_recv.at[slot], partner)
 
     def accumulate(rs, p):
         lhs = jnp.concatenate([got[blk(r), p] for r in rs], axis=0)
@@ -747,11 +778,13 @@
                 kv_ref[b, kind - 1] = made
 
     def share(r):
-        for ahead in range(1, tracts):
-
-            @pl.when(tract + ahead < tracts)
-            def _():
-                kv_copy(ahead, blk(r)).start()
+        @pl.when(tract < 2)
+        def _():
+            kv_far(blk(r)).start()
+
+        @pl.when(core == 0)
+        def _():
+            kv_near(blk(r)).start()
 
     acc_ref[...] = jnp.zeros_like(acc_ref)
     own_load.wait()
@@ -761,21 +794,34 @@
         power += jnp.sum(tokens * tokens, axis=-1, keepdims=True)
     table_load.wait()
     factor = lax.rsqrt(power * (1.0 / width) + 1e-06)
+    pl.semaphore_wait(barrier, n - 1 + seats - 1)
+
+    @pl.when(is_end)
+    def _():
+        for kind in (1, 2, 0):
+            far_first(kind).start()
+
+    def send_own(p):
+        @pl.when(is_end)
+        def _():
+            tok(0, 0, p).start()
+
+        @pl.when(is_helper)
+        def _():
+            tok(0, 1, p).start()
+            if p < near:
+                tok(1, 1, p).start()
+
     for p in range(pieces):
         tokens = raw[:, p * deep : (p + 1) * deep].astype(jnp.float32)
         shaped = tokens * factor * (1.0 + style(1, p * deep)) + style(0, p * deep)
         got[me, p] = shaped.astype(got.dtype)
-    pl.semaphore_wait(barrier, n - 1 + seats - 1)
+        if p:
+            send_own(p - 1)
+    send_own(pieces - 1)
 
     @pl.when(is_end)
     def _():
-        for kind in (1, 2, 0):
-            far_first(kind).start()
-
-        @pl.loop(0, pieces)
-        def _(j):
-            tok(0, 0, lax.rem(j + near, pieces)).start()
-
         @pl.loop(0, pieces)
         def _(p):
             wq_load(p).wait()
@@ -815,14 +861,9 @@
 
     @pl.when(is_helper)
     def _():
-        @pl.loop(0, near)
-        def _(p):
-            tok(0, 1, p).start()
-            tok(1, 1, p).start()
-
-        @pl.loop(near, pieces)
-        def _(p):
-            tok(0, 1, p).start()
+        def pass_on(p):
+            tok(0, 0, p).wait_recv()
+            tok(0, 0, p).start()
 
         @pl.loop(0, pieces)
         def _(p):
@@ -840,9 +881,15 @@
                 def _():
                     far_relay(kind)
 
-            @pl.when(p == pieces - 2)
-            def _():
-                far_hand(1)
+            for at, kind in ((4, 1), (6, 2)):
+
+                @pl.when(p == at)
+                def _():
+                    far_hand_x(kind)
+
+            @pl.when(p >= pieces - 2)
+            def _():
+                pass_on(p - (pieces - 2))
 
         settle(1, (1, 2, 0))
         share(1)
@@ -850,26 +897,14 @@
         share(2)
         for cut in range(cuts):
             wo_load(cut).wait()
-        wo_start(1, 1, range(cuts))
-        far_ready(1)
-        far_part((1, 2), (1,))
-
-        def pass_on(j):
-            p = lax.rem(j + near, pieces)
-            tok(0, 0, p).wait_recv()
-            tok(0, 0, p).start()
-
-        @pl.loop(0, 2)
-        def _(j):
-            pass_on(j)
+        wo_start(1, 1, range(cuts - 1))
 
         @pl.loop(0, pieces)
-        def _(j):
-            @pl.when(j + 2 < pieces)
-            def _():
-                pass_on(j + 2)
-
-            p = lax.rem(j + near, pieces)
+        def _(p):
+            @pl.when(p + 2 < pieces)
+            def _():
+                pass_on(p + 2)
+
             tok(1, 3, p).wait_recv()
 
             @pl.when(p < near)
@@ -878,35 +913,45 @@
 
             accumulate((0, 3), p)
 
-            @pl.when(j == 2)
-            def _():
-                far_hand(2)
-
-            @pl.when(j == 3)
+            @pl.when(p == 0)
+            def _():
+                far_hand_x(0)
+
+            @pl.when(p == 1)
+            def _():
+                far_hand_y(1)
+                far_ready(1)
+                far_part((1, 2), (1,))
+
+            @pl.when(p == 3)
+            def _():
+                far_hand_y(2)
+
+            @pl.when(p == 4)
             def _():
                 far_ready(2)
                 far_part((1, 2), (2,))
 
-            @pl.when(j == 5)
-            def _():
-                far_hand(0)
-                far_part((3,), (1, 2))
-                far_ready(0)
-                far_part((1, 2, 3), (0,))
-
+            @pl.when(p == 6)
+            def _():
+                far_hand_y(0)
+
+        far_part((3,), (1, 2))
         settle(0, (1, 2, 0))
         share(0)
         settle(3, (1, 2, 0))
         share(3)
-        for cut in range(cuts - 1):
-            wo_start(0, 1, (cut,))
-            wo_forward(0, 0, cut)
+        far_ready(0)
+        far_part((1, 2, 3), (0,))
+        wo_start(1, 1, (cuts - 1,))
+        for way, r, cut in along[:early]:
+            wo_next(way, r, cut)
 
     tokens_here = n * rows
     heads_here = q_ref.shape[2] // HD
     scale = HD ** (-0.5)
 
-    def attend(source, allowed):
+    def attend(source, bias):
         for head in range(heads_here):
             lanes = slice(head * HD, (head + 1) * HD)
             queries = q_ref[:, :, lanes].reshape(tokens_here, HD)
@@ -914,24 +959,26 @@
             values = source[:, 1, :, lanes].reshape(tokens_here, HD)
             scores = (
                 lax.dot_general(
-                    queries, keys, (((1,), (1,)), ((), ())), preferred_element_type=jnp.float32
+                    keys, queries, (((1,), (1,)), ((), ())), preferred_element_type=jnp.float32
                 )
                 * scale
             )
-            if allowed is None:
-                peak = jnp.max(scores, axis=1, keepdims=True)
-                probs = jnp.exp(scores - peak)
-            else:
-                scores = jnp.where(allowed, scores, -1e30)
+            if bias is not None:
+                scores = scores + bias
+            peak = jnp.max(scores, axis=0, keepdims=True)
+            if bias is not None:
                 old = peak_ref[head]
-                peak = jnp.maximum(old, jnp.max(scores, axis=1, keepdims=True))
-                probs = jnp.where(allowed, jnp.exp(scores - peak), 0.0)
+                peak = jnp.maximum(old, peak)
+            probs = jnp.exp(scores - peak)
+            row_sum = jnp.sum(probs, axis=0, keepdims=True)
+            weighted = lax.dot_general(
+                values,
+                probs.astype(jnp.bfloat16),
+                (((0,), (0,)), ((), ())),
+                preferred_element_type=jnp.float32,
+            )
+            if bias is not None:
                 rescale = jnp.exp(old - peak)
-            row_sum = jnp.sum(probs, axis=1, keepdims=True)
-            weighted = jnp.dot(
-                probs.astype(jnp.bfloat16), values, preferred_element_type=jnp.float32
-            )
-            if allowed is not None:
                 row_sum += sum_ref[head] * rescale
                 weighted += mix_ref[head] * rescale
             peak_ref[head] = peak
@@ -940,18 +987,22 @@
 
     attend(kv_ref, None)
 
-    for ahead in range(1, tracts):
+    @pl.when(tract >= 2)
+    def _():
+        kv_slot(1).wait_recv()
+        kv_relay().start()
+
+    for ahead in (2, 1, 3):
 
         @pl.when(tract >= ahead)
         def _():
-            @pl.loop(0, n)
-            def _(block):
-                kv_copy(ahead, block).wait_recv()
-
-            attend(kv_in.at[ahead - 1], visible_ref[0, lax.max(tract - ahead, 0)] > 0)
+            if ahead != 2:
+                kv_slot(ahead - 1).wait_recv()
+            seen = visible_ref[0, lax.max(tract - ahead, 0)] > 0
+            attend(kv_in.at[ahead - 1], jnp.where(seen, 0.0, -1e30))
 
     for head in range(heads_here):
-        attended = (mix_ref[head] / sum_ref[head]).astype(jnp.bfloat16)
+        attended = jnp.transpose(mix_ref[head] / sum_ref[head]).astype(jnp.bfloat16)
         att_ref[:, :, head * HD : (head + 1) * HD] = attended.reshape(n, rows, HD)
 
     def att_line(other, source):
@@ -963,6 +1014,10 @@
             {"head": other},
         )
 
+    def att_passed(by, side):
+        ref = att_all.at[chip_at(chips - by) * 2 + side]
+        return remote(ref, ref, a_send.at[chips + by], b_recv.at[by], partner)
+
     for ahead in range(1, n):
         other = lax.rem(me + ahead, n)
         att_line(other, me).start()
@@ -970,20 +1025,19 @@
 
     @pl.when(is_helper)
     def _():
-        wo_start(0, 1, (cuts - 1,))
-        wo_forward(0, 0, cuts - 1)
-        for cut in range(cuts - 1):
-            for r in (2, 3):
-                wo_forward(1, r, cut)
+        for way, r, cut in along[early:]:
+            wo_next(way, r, cut)
+        for way, r, cut in back[:early]:
+            wo_next(way, r, cut)
 
     def att_chip(by, z, which):
         ref = att_all.at[which * 2 + core, z]
-        return remote(ref, ref, a_send.at[by, z], a_recv.at[by, z], place(chip_at(by), core))
+        return remote(ref, ref, a_send.at[by], a_recv.at[by, z], place(chip_at(by), core))
 
     def att_pass(by, z, side):
         ref = att_all.at[chip_at(chips - by) * 2 + side, z]
         where = chips + by
-        return remote(ref, ref, a_send.at[where, z], a_recv.at[where, z], partner)
+        return remote(ref, ref, a_send.at[where], b_recv.at[by], partner)
 
     for ahead in range(n):
         z = lax.rem(me + ahead, n)
@@ -993,26 +1047,31 @@
             att_chip(by, z, chip).start()
         att_pass(0, z, core).start()
 
-    @pl.when(is_helper)
-    def _():
-        for r in (2, 3):
-            wo_forward(1, r, cuts - 1)
-
     for ahead in range(n):
         z = lax.rem(me + ahead, n)
         for by in range(1, chips):
             att_chip(by, z, chip_at(chips - by)).wait_recv()
             att_pass(by, z, core).start()
-
-    for z in range(n):
-        for by in range(chips):
-            att_pass(by, z, 1 - core).wait_recv()
+        if ahead == 1:
+
+            @pl.when(is_helper)
+            def _():
+                for move in back[2:3]:
+                    wo_next(*move)
+
+    @pl.when(is_helper)
+    def _():
+        for move in back[3:4]:
+            wo_next(*move)
+
+    for by in range(chips):
+        att_passed(by, 1 - core).wait_recv()
 
     def out_copy(which, side, source, cut):
         return remote(
             out_part.at[which * 2 + side, cut],
             out_in.at[source, cut],
-            o_send.at[which * 2 + side, cut],
+            o_send.at[which * 2 + side],
             o_recv.at[source, cut],
             place(which, side),
         )
@@ -1025,6 +1084,12 @@
         def _():
             for r in (1, 2, 3):
                 wo_copy(0, r, cut).wait_recv()
+
+        @pl.when(is_helper)
+        def _():
+            for way, r, at in back[4:]:
+                if cut == (max(0, at - 2) if r == 2 else at):
+                    wo_next(way, r, at)
 
         total = None
         for z in range(n):
@@ -1049,63 +1114,54 @@
             out_copy(chip, core, source, cut).wait_recv()
             finish(out_in, source, cut)
 
-    for cut in range(cuts):
-        for by, side in others:
-            lane = core if side == 0 else 1 - core
-            out_copy(chip_at(by), lane, seat, cut).wait_send()
-    for z in range(n):
-        for by in range(1, chips):
-            att_chip(by, z, chip).wait_send()
-        for by in range(chips):
-            att_pass(by, z, core).wait_send()
+    for by, side in others:
+        lane = core if side == 0 else 1 - core
+        target = chip_at(by) * 2 + lane
+        ref = out_part.at[target]
+        sems = o_send.at[target], o_recv.at[seat, 0]
+        remote(ref, out_in.at[seat], *sems, place(chip_at(by), lane)).wait_send()
+    for by in range(chips):
+        if by:
+            ref = att_all.at[seat]
+            remote(ref, ref, a_send.at[by], a_recv.at[by, 0], partner).wait_send()
+        att_passed(by, core).wait_send()
     for ahead in range(1, n):
         att_line(lax.rem(me + ahead, n), me).wait_send()
-
-    @pl.loop(0, n)
-    def _(block):
-        for ahead in range(1, tracts):
-
-            @pl.when(tract + ahead < tracts)
-            def _():
-                kv_copy(ahead, block).wait_send()
+    for slot, used in ((0, core == 0), (1, tract < 2), (2, tract >= 2)):
+
+        @pl.when(used)
+        def _():
+            kv_slot(slot).wait_send()
+
+    def far_sent(where, which):
+        ref = w_far.at[:, far_span(which, core)]
+        remote(ref, ref, f_send.at[where], f_recv.at[where, 0], partner).wait_send()
+
+    def wo_sent(way, r):
+        ref = wo_ref.at[blk(r)]
+        remote(ref, ref, wo_send.at[way, blk(r)], wo_recv.at[blk(r), 0], partner).wait_send()
 
     @pl.when(is_end)
     def _():
-        for kind in range(3):
-            far_first(kind).wait_send()
-
-        @pl.loop(0, pieces)
-        def _(p):
-            tok(0, 0, p).wait_send()
-
-        for cut in range(cuts):
-            wo_copy(0, 0, cut).wait_send()
+        far_sent(0, chip)
+        tok_sent(0, 0, pieces)
+        wo_sent(0, 0)
 
     @pl.when(is_helper)
     def _():
-        for kind in range(3):
-            for by in range(1, chips):
-                far_out(by, kind).wait_send()
-            for by in range(chips):
-                far_pass(by, kind, core).wait_send()
-            for r in (1, 2, 3):
-                part_copy(r, kind).wait_send()
-
-        @pl.loop(0, pieces)
-        def _(p):
-            for r in (0, 1):
-                tok(0, r, p).wait_send()
-
-        @pl.loop(0, near)
-        def _(p):
-            for r in (1, 2, 3):
-                tok(1, r, p).wait_send()
-
-        for cut in range(cuts):
-            for r in (0, 1):
-                wo_copy(0, r, cut).wait_send()
-            for r in (1, 2, 3):
-                wo_copy(1, r, cut).wait_send()
+        for slot in range(chips):
+            if slot:
+                far_sent(slot, across[1] if slot == 3 else chip)
+            far_sent(chips + slot, across[slot])
+        for r in (1, 2, 3):
+            ref = part_ref.at[blk(r)]
+            sems = p_send.at[blk(r)], p_recv.at[blk(r), 0]
+            remote(ref, ref, *sems, partner).wait_send()
+            tok_sent(1, r, near)
+            wo_sent(1, r)
+        for r in (0, 1):
+            tok_sent(0, r, pieces)
+            wo_sent(0, r)
 
 
 PIECES = 8
@@ -1118,8 +1174,7 @@
     far = (PIECES - NEAR) * (width // PIECES)
     return (
         n == 4
-        and tracts % 2 == 0
-        and seats > 2
+        and (tracts, reps) == (4, 2)
         and rows % 16 == 0
         and width % (PIECES * 128) == 0
         and width % (seats * 256) == 0
@@ -1162,30 +1217,31 @@
             pltpu.VMEM((n, 3, rows, cols), half),
             pltpu.VMEM((n, 3, rows, cols), half),
             pltpu.VMEM((n, rows, cols), half),
-            pltpu.VMEM((heads_here, n * rows, 1), jnp.float32),
-            pltpu.VMEM((heads_here, n * rows, 1), jnp.float32),
-            pltpu.VMEM((heads_here, n * rows, HD), jnp.float32),
+            pltpu.VMEM((heads_here, 1, n * rows), jnp.float32),
+            pltpu.VMEM((heads_here, 1, n * rows), jnp.float32),
+            pltpu.VMEM((heads_here, HD, n * rows), jnp.float32),
             pltpu.VMEM((seats, n, rows, cols), half),
             pltpu.VMEM((seats, cuts, rows, 256), half),
             pltpu.VMEM((seats, cuts, rows, 256), half),
             dma((2,)),
             dma((PIECES,)),
             dma((cuts,)),
-            dma((2, n, PIECES)),
+            dma((2, n)),
             dma((n, PIECES)),
+            dma((2 * chips,)),
             dma((2 * chips, 3)),
-            dma((2 * chips, 3)),
+            dma((n,)),
             dma((n, 3)),
-            dma((n, 3)),
-            dma((tracts, n)),
-            dma((tracts, n)),
-            dma((2, n, cuts)),
+            dma((tracts,)),
+            dma((tracts,)),
+            dma((2, n)),
             dma((n, cuts)),
             dma((n,)),
             dma((n,)),
-            dma((2 * chips, n)),
-            dma((2 * chips, n)),
-            dma((seats, cuts)),
+            dma((2 * chips,)),
+            dma((chips, n)),
+            dma((chips,)),
+            dma((seats,)),
             dma((seats, cuts)),
         ],
         compiler_params=pltpu.CompilerParams(

time: 85.6 us -> 80.1 us (0.936)
  Pallas kernels: 83.9 us -> 78.4 us
    pallas_call x1, Pallas kernels: 83.9 us -> 78.4 us  [line_body(): pl.pallas_call(functools.partial(line_kernel, n, tracts, reps, PIECES, NE...]
where the time goes in v2:
time: 80.1 us; the launch traced here: 80 us
  Pallas kernels  78.4 us (98%)
  local copies, waits for them, and re-layouts  0.88 us (1%)
    pallas_call x1, Pallas kernels, line_body(): pl.pallas_call(functools.partial(line_kernel, n, tracts, reps, PIECES, NE...  78.4 us

profile of v2, /device:TPU:0, one launch (start us, length us, event | category | flops | bytes accessed | tf_op | source)
XLA Modules:
  0.0 80.0 jit_solution(5699458772407297691)
XLA Ops:
  0.7 78.4 %shard_map.64 = bf16[1,64,6144]{2,1,0:T(8,128)(2,1)S(1)} custom-call(bf16[1,64,6144]{2,1,0:T(8,128)(2,1)} %x_ref.1, s32[1]{0:T(128)S(6)} %copy.9.level_ref, s32[1,4]{1,0:T(1,128)} %visible_ref.1, bf16[3,6144,256]{2,1,0:T(8,128)(2,1)} %bitcast.2, bf16[256,6144]{1,0:T(8,128)(2,1)} %out_hbm.1, f32[3,8,6144]{2,1,0:T(8,128)} %bitcast.3), custom_call_target="tpu_custom_call" | custom-call | tf_op jit(solution)/shard_map/pallas_call | solution.py:1201
  79.1 0.9 %copy.8 = bf16[1,64,6144]{2,1,0:T(8,128)(2,1)} copy(bf16[1,64,6144]{2,1,0:T(8,128)(2,1)S(1)} %shard_map.64) | data formatting | bytes 1572864

commit v3 on v2

--- a/solution.py
+++ b/solution.py
@@ -579,6 +579,19 @@
     def place(which, side):
         return {"rep": which // wide, "tract": lax.rem(which, wide) * 2 + side}
 
+    across = [
+        chip,
+        rep * wide + 1 - lax.rem(chip, wide),
+        (1 - rep) * wide + lax.rem(chip, wide),
+        (1 - rep) * wide + 1 - lax.rem(chip, wide),
+    ]
+    along_x, along_y = place(across[1], core), place(across[2], core)
+    others = [(by, side) for by in (1, 2, 3) for side in (0, 1)] + [(0, 1)]
+
+    def seat_of(by, side):
+        return across[(3, 1, 2)[by - 1] if by else 0], core if side == 0 else 1 - core
+
+
     own_load = pltpu.make_async_copy(x_ref.at[0], raw, load_sem.at[0])
     own_load.start()
     table_load = pltpu.make_async_copy(table_hbm, table_ref, load_sem.at[1])
@@ -592,6 +605,9 @@
         src = out_hbm.at[:, pl.ds(start, cut_cols)]
         return pltpu.make_async_copy(src, wo_ref.at[me, cut], wo_sem.at[cut])
 
+    def wo_loaded():
+        for cut in range(cuts):
+            wo_load(cut).wait()
 
     def wq_load(p):
         span = pl.ds(pl.multiple_of(p * deep, deep), deep)
@@ -608,12 +624,9 @@
     for ahead in range(1, n):
         other = lax.rem(me + ahead, n)
         pl.semaphore_signal(barrier, inc=1, device_id={"head": other}, device_id_type=MESH)
-    for by in range(chips):
-        for side in range(2):
-            if by == 0 and side == 1:
-                continue
-            target = partner if by == 0 else place(chip_at(by), side)
-            pl.semaphore_signal(barrier, inc=1, device_id=target, device_id_type=MESH)
+    for other in others:
+        target = place(*seat_of(*other))
+        pl.semaphore_signal(barrier, inc=1, device_id=target, device_id_type=MESH)
 
     level = level_ref[0]
 
@@ -654,14 +667,6 @@
         src = w_hbm.at[kind, pl.ds(pl.multiple_of(start, far_rows), far_rows)]
         dst = w_far.at[kind, far_span(chip, core)]
         return remote(src, dst, f_send.at[0], f_recv.at[0, kind], inner)
-
-    across = [
-        chip,
-        rep * wide + 1 - lax.rem(chip, wide),
-        (1 - rep) * wide + lax.rem(chip, wide),
-        (1 - rep) * wide + 1 - lax.rem(chip, wide),
-    ]
-    along_x, along_y = place(across[1], core), place(across[2], core)
 
     def far_move(slot, kind, which):
         ref = w_far.at[kind, far_span(which, core)]
@@ -718,29 +723,35 @@
             for kind in kinds:
                 part_copy(r, kind).start()
 
-    def wo_copy(way, r, cut):
+    halves = wo_recv.shape[2]
+    half_rows = wo_ref.shape[2] // halves
+
+    def wo_copy(way, r, cut, half):
         b = blk(r)
-        ref = wo_ref.at[b, cut]
+        ref = wo_ref.at[b, cut, pl.ds(half * half_rows, half_rows)]
         target = inner if way == 0 else outer
-        return remote(ref, ref, wo_send.at[way, b], wo_recv.at[b, cut], target)
+        return remote(ref, ref, wo_send.at[way, b], wo_recv.at[b, cut, half], target)
 
     def wo_start(way, r, which):
         for cut in which:
-            wo_copy(way, r, cut).start()
+            for half in range(halves):
+                wo_copy(way, r, cut, half).start()
 
     along = [(0, r, cut) for cut in range(cuts) for r in (1, 0)]
     back = [(1, r, cut) for cut in range(cuts) for r in (2, 3)]
     early = 2
 
     def wo_next(way, r, cut):
-        if r == 1:
-            wo_start(way, r, (cut,))
-        else:
-            wo_forward(way, r, cut)
-
-    def wo_forward(way, r, cut):
-        wo_copy(way, r, cut).wait_recv()
-        wo_copy(way, r, cut).start()
+        for half in range(halves):
+            if r != 1:
+                wo_copy(way, r, cut, half).wait_recv()
+            wo_copy(way, r, cut, half).start()
+
+    def wo_moves(*moves):
+        @pl.when(is_helper)
+        def _():
+            for move in moves:
+                wo_next(*move)
 
     def kv_near(b):
         ref, slot = kv_ref.at[b], kv_in.at[0, b]
@@ -794,17 +805,19 @@
         power += jnp.sum(tokens * tokens, axis=-1, keepdims=True)
     table_load.wait()
     factor = lax.rsqrt(power * (1.0 / width) + 1e-06)
-    pl.semaphore_wait(barrier, n - 1 + seats - 1)
+    pl.semaphore_wait(barrier, n - 1 + len(others))
 
     @pl.when(is_end)
     def _():
-        for kind in (1, 2, 0):
+        for kind in (1, 2):
             far_first(kind).start()
 
     def send_own(p):
         @pl.when(is_end)
         def _():
             tok(0, 0, p).start()
+            if p == 0:
+                far_first(0).start()
 
         @pl.when(is_helper)
         def _():
@@ -827,8 +840,7 @@
             wq_load(p).wait()
             accumulate((0,), p)
 
-        for cut in range(cuts):
-            wo_load(cut).wait()
+        wo_loaded()
         wo_start(0, 0, range(cuts))
 
         settle(0, (1, 2, 0))
@@ -864,6 +876,7 @@
         def pass_on(p):
             tok(0, 0, p).wait_recv()
             tok(0, 0, p).start()
+            accumulate((0,), p)
 
         @pl.loop(0, pieces)
         def _(p):
@@ -875,11 +888,16 @@
                 tok(1, 2, p).start()
 
             accumulate((1, 2), p)
-            for at, kind in ((1, 1), (3, 2), (5, 0)):
+            for at, kind in ((1, 1), (3, 2), (7, 0)):
 
                 @pl.when(p == at)
                 def _():
                     far_relay(kind)
+
+            @pl.when(p == near)
+            def _():
+                wo_loaded()
+                wo_start(1, 1, range(cuts - 1))
 
             for at, kind in ((4, 1), (6, 2)):
 
@@ -895,9 +913,6 @@
         share(1)
         settle(2, (1, 2, 0))
         share(2)
-        for cut in range(cuts):
-            wo_load(cut).wait()
-        wo_start(1, 1, range(cuts - 1))
 
         @pl.loop(0, pieces)
         def _(p):
@@ -905,21 +920,26 @@
             def _():
                 pass_on(p + 2)
 
+            @pl.when(p == pieces - 1)
+            def _():
+                far_ready(0)
+                far_part((1, 2), (0,))
+
             tok(1, 3, p).wait_recv()
 
             @pl.when(p < near)
             def _():
                 tok(1, 3, p).start()
 
-            accumulate((0, 3), p)
-
-            @pl.when(p == 0)
+            accumulate((3,), p)
+
+            @pl.when(p == 1)
+            def _():
+                far_hand_y(1)
+
+            @pl.when(p == 2)
             def _():
                 far_hand_x(0)
-
-            @pl.when(p == 1)
-            def _():
-                far_hand_y(1)
                 far_ready(1)
                 far_part((1, 2), (1,))
 
@@ -931,19 +951,21 @@
             def _():
                 far_ready(2)
                 far_part((1, 2), (2,))
-
-            @pl.when(p == 6)
+                wo_start(1, 1, (cuts - 1,))
+
+            @pl.when(p == 5)
+            def _():
+                settle(0, (1, 2, 0))
+                share(0)
+
+            @pl.when(p == 5)
             def _():
                 far_hand_y(0)
 
-        far_part((3,), (1, 2))
-        settle(0, (1, 2, 0))
-        share(0)
-        settle(3, (1, 2, 0))
+        far_part((3,), (1, 2, 0))
+        settle(3, (1, 2))
         share(3)
-        far_ready(0)
-        far_part((1, 2, 3), (0,))
-        wo_start(1, 1, (cuts - 1,))
+        settle(3, (0,))
         for way, r, cut in along[:early]:
             wo_next(way, r, cut)
 
@@ -993,6 +1015,11 @@
         kv_relay().start()
 
     for ahead in (2, 1, 3):
+        if ahead == 3:
+
+            @pl.when(is_helper)
+            def _():
+                wo_next(*back[0])
 
         @pl.when(tract >= ahead)
         def _():
@@ -1014,82 +1041,81 @@
             {"head": other},
         )
 
-    def att_passed(by, side):
-        ref = att_all.at[chip_at(chips - by) * 2 + side]
-        return remote(ref, ref, a_send.at[chips + by], b_recv.at[by], partner)
-
     for ahead in range(1, n):
         other = lax.rem(me + ahead, n)
         att_line(other, me).start()
     att_all[seat, me] = att_ref[me]
 
+    def att_chip(by, z, which):
+        ref = att_all.at[which * 2 + core] if z is None else att_all.at[which * 2 + core, z]
+        at = a_recv.at[by, 0 if z is None else z]
+        return remote(ref, ref, a_send.at[by], at, place(seat_of(by, 0)[0], core))
+
+    def att_pass(by, z, side):
+        owner = seat_of(by, 0)[0] * 2 + side
+        ref = att_all.at[owner] if z is None else att_all.at[owner, z]
+        return remote(ref, ref, a_send.at[chips + by], b_recv.at[by], partner)
+
     @pl.when(is_helper)
     def _():
-        for way, r, cut in along[early:]:
-            wo_next(way, r, cut)
-        for way, r, cut in back[:early]:
-            wo_next(way, r, cut)
-
-    def att_chip(by, z, which):
-        ref = att_all.at[which * 2 + core, z]
-        return remote(ref, ref, a_send.at[by], a_recv.at[by, z], place(chip_at(by), core))
-
-    def att_pass(by, z, side):
-        ref = att_all.at[chip_at(chips - by) * 2 + side, z]
-        where = chips + by
-        return remote(ref, ref, a_send.at[where], b_recv.at[by], partner)
-
-    for ahead in range(n):
-        z = lax.rem(me + ahead, n)
+        for move in along[early:]:
+            wo_next(*move)
+
+    line = [blk(jnp.where(is_end, end, help)) for end, help in ((0, 1), (1, 2), (2, 0), (3, 3))]
+
+    for ahead, z in enumerate(line):
         if ahead:
             att_line(z, z).wait_recv()
         for by in range(1, chips):
             att_chip(by, z, chip).start()
         att_pass(0, z, core).start()
-
-    for ahead in range(n):
-        z = lax.rem(me + ahead, n)
+        if ahead < 2:
+            wo_moves(back[1 + ahead])
+
+    wo_moves(*back[3:4])
+    for z in line:
         for by in range(1, chips):
-            att_chip(by, z, chip_at(chips - by)).wait_recv()
+            att_chip(by, z, seat_of(by, 0)[0]).wait_recv()
             att_pass(by, z, core).start()
-        if ahead == 1:
-
-            @pl.when(is_helper)
-            def _():
-                for move in back[2:3]:
-                    wo_next(*move)
-
-    @pl.when(is_helper)
-    def _():
-        for move in back[3:4]:
-            wo_next(*move)
-
+    wo_moves(*back[4:5])
     for by in range(chips):
-        att_passed(by, 1 - core).wait_recv()
-
-    def out_copy(which, side, source, cut):
+        att_pass(by, None, 1 - core).wait_recv()
+
+    def out_copy(by, side, source, cut):
+        which, lane = seat_of(by, side)
         return remote(
-            out_part.at[which * 2 + side, cut],
+            out_part.at[which * 2 + lane, cut],
             out_in.at[source, cut],
-            o_send.at[which * 2 + side],
+            o_send.at[which * 2 + lane],
             o_recv.at[source, cut],
-            place(which, side),
+            place(which, lane),
         )
 
-    others = [(by, side) for by in range(1, chips) for side in range(2)] + [(0, 1)]
     heads_wide = wo_ref.shape[2]
+
+    def finish(ref, source, cut):
+        span = pl.ds(pl.multiple_of(source * cols_out + cut * cut_cols, 128), cut_cols)
+        gate = table_ref[2, pl.ds(level, 1), span]
+        done = ref[source, cut].astype(jnp.float32) * gate
+        out_ref[0, :, span] = done.astype(out_ref.dtype)
+
+    def finish_cut(cut):
+        finish(out_part, seat, cut)
+        for by, side in reversed(others):
+            which, lane = seat_of(by, side)
+            source = which * 2 + lane
+            out_copy(by, side, source, cut).wait_recv()
+            finish(out_in, source, cut)
+
     for cut in range(cuts):
 
         @pl.when(is_end)
         def _():
+            if cut == 2:
+                finish_cut(0)
             for r in (1, 2, 3):
-                wo_copy(0, r, cut).wait_recv()
-
-        @pl.when(is_helper)
-        def _():
-            for way, r, at in back[4:]:
-                if cut == (max(0, at - 2) if r == 2 else at):
-                    wo_next(way, r, at)
+                for half in range(halves):
+                    wo_copy(0, r, cut, half).wait_recv()
 
         total = None
         for z in range(n):
@@ -1098,33 +1124,28 @@
             total = made if total is None else total + made
         out_part[:, cut] = total.astype(out_part.dtype).reshape(seats, rows, cut_cols)
         for by, side in others:
-            lane = core if side == 0 else 1 - core
-            out_copy(chip_at(by), lane, seat, cut).start()
-
-    def finish(ref, source, cut):
-        span = pl.ds(pl.multiple_of(source * cols_out + cut * cut_cols, 128), cut_cols)
-        gate = table_ref[2, pl.ds(level, 1), span]
-        out_ref[0, :, span] = (ref[source, cut].astype(jnp.float32) * gate).astype(out_ref.dtype)
+            out_copy(by, side, seat, cut).start()
+        if cut == 0:
+            wo_moves(*back[5:])
 
     for cut in range(cuts):
-        finish(out_part, seat, cut)
-        for by, side in others:
-            lane = core if side == 0 else 1 - core
-            source = chip_at(chips - by) * 2 + lane
-            out_copy(chip, core, source, cut).wait_recv()
-            finish(out_in, source, cut)
+        if cut == 0 and cuts > 2:
+
+            @pl.when(is_helper)
+            def _():
+                finish_cut(0)
+        else:
+            finish_cut(cut)
 
     for by, side in others:
-        lane = core if side == 0 else 1 - core
-        target = chip_at(by) * 2 + lane
-        ref = out_part.at[target]
-        sems = o_send.at[target], o_recv.at[seat, 0]
-        remote(ref, out_in.at[seat], *sems, place(chip_at(by), lane)).wait_send()
+        which, lane = seat_of(by, side)
+        to = which * 2 + lane
+        sems = o_send.at[to], o_recv.at[seat, 0]
+        remote(out_part.at[to], out_in.at[seat], *sems, partner).wait_send()
     for by in range(chips):
         if by:
-            ref = att_all.at[seat]
-            remote(ref, ref, a_send.at[by], a_recv.at[by, 0], partner).wait_send()
-        att_passed(by, core).wait_send()
+            att_chip(by, None, chip).wait_send()
+        att_pass(by, None, core).wait_send()
     for ahead in range(1, n):
         att_line(lax.rem(me + ahead, n), me).wait_send()
     for slot, used in ((0, core == 0), (1, tract < 2), (2, tract >= 2)):
@@ -1139,7 +1160,8 @@
 
     def wo_sent(way, r):
         ref = wo_ref.at[blk(r)]
-        remote(ref, ref, wo_send.at[way, blk(r)], wo_recv.at[blk(r), 0], partner).wait_send()
+        sems = wo_send.at[way, blk(r)], wo_recv.at[blk(r), 0, 0]
+        remote(ref, ref, *sems, partner).wait_send()
 
     @pl.when(is_end)
     def _():
@@ -1235,7 +1257,7 @@
             dma((tracts,)),
             dma((tracts,)),
             dma((2, n)),
-            dma((n, cuts)),
+            dma((n, cuts, 2)),
             dma((n,)),
             dma((n,)),
             dma((2 * chips,)),

time: 80.1 us -> 76.5 us (0.955)
  Pallas kernels: 78.4 us -> 74.8 us
    pallas_call x1, Pallas kernels: 78.4 us -> 74.8 us  [line_body(): pl.pallas_call(functools.partial(line_kernel, n, tracts, reps, PIECES, NE...]
where the time goes in v3:
time: 76.5 us; the launch traced here: 76.4 us
  Pallas kernels  74.8 us (98%)
  local copies, waits for them, and re-layouts  0.88 us (1%)
    pallas_call x1, Pallas kernels, line_body(): pl.pallas_call(functools.partial(line_kernel, n, tracts, reps, PIECES, NE...  74.8 us

profile of v3, /device:TPU:0, one launch (start us, length us, event | category | flops | bytes accessed | tf_op | source)
XLA Modules:
  0.0 76.4 jit_solution(3743978485023058383)
XLA Ops:
  0.7 74.8 %shard_map.64 = bf16[1,64,6144]{2,1,0:T(8,128)(2,1)S(1)} custom-call(bf16[1,64,6144]{2,1,0:T(8,128)(2,1)} %x_ref.1, s32[1]{0:T(128)S(6)} %copy.9.level_ref, s32[1,4]{1,0:T(1,128)} %visible_ref.1, bf16[3,6144,256]{2,1,0:T(8,128)(2,1)} %bitcast.2, bf16[256,6144]{1,0:T(8,128)(2,1)} %out_hbm.1, f32[3,8,6144]{2,1,0:T(8,128)} %bitcast.3), custom_call_target="tpu_custom_call" | custom-call | tf_op jit(solution)/shard_map/pallas_call | solution.py:1223
  75.5 0.9 %copy.8 = bf16[1,64,6144]{2,1,0:T(8,128)(2,1)} copy(bf16[1,64,6144]{2,1,0:T(8,128)(2,1)S(1)} %shard_map.64) | data formatting | bytes 1572864

commit v4 on v3

--- a/solution.py
+++ b/solution.py
@@ -514,6 +514,7 @@
     table_hbm,
     out_ref,
     table_ref,
+    gate_ref,
     raw,
     got,
     wq_ref,
@@ -533,7 +534,6 @@
     out_part,
     out_in,
     load_sem,
-    wq_sem,
     wo_sem,
     g_send,
     g_recv,
@@ -597,28 +597,23 @@
     table_load = pltpu.make_async_copy(table_hbm, table_ref, load_sem.at[1])
     table_load.start()
     cols_out = width // seats
-    cuts = wo_ref.shape[1]
-    cut_cols = cols_out // cuts
-
-    def wo_load(cut):
-        start = pl.multiple_of(seat * cols_out + cut * cut_cols, 128)
-        src = out_hbm.at[:, pl.ds(start, cut_cols)]
-        return pltpu.make_async_copy(src, wo_ref.at[me, cut], wo_sem.at[cut])
+    units = wo_ref.shape[1]
+    cuts, unit = units // 2, cols_out // units
+
+    def wo_load(k):
+        start = pl.multiple_of(seat * cols_out + k * unit, 128)
+        src = out_hbm.at[:, pl.ds(start, unit)]
+        return pltpu.make_async_copy(src, wo_ref.at[me, k], wo_sem.at[k])
 
     def wo_loaded():
-        for cut in range(cuts):
-            wo_load(cut).wait()
-
-    def wq_load(p):
-        span = pl.ds(pl.multiple_of(p * deep, deep), deep)
-        return pltpu.make_async_copy(w_hbm.at[:, span], wq_ref.at[:, span], wq_sem.at[p])
-
-    @pl.loop(0, pieces)
-    def _(p):
-        wq_load(p).start()
-
-    for cut in range(cuts):
-        wo_load(cut).start()
+        for k in range(units):
+            wo_load(k).wait()
+
+    wq_load = pltpu.make_async_copy(w_hbm, wq_ref, load_sem.at[2])
+    wq_load.start()
+
+    for k in range(units):
+        wo_load(k).start()
 
     barrier = pltpu.get_barrier_semaphore()
     for ahead in range(1, n):
@@ -643,17 +638,28 @@
             device_id_type=MESH,
         )
 
-    def tok(way, r, p):
+    parts = g_recv.shape[2]
+    part_rows = rows // parts
+
+    def tok(way, r, p, part):
         b = blk(r)
-        ref = got.at[b, p]
+        ref = got.at[b, p, pl.ds(part * part_rows, part_rows)]
         target = inner if way == 0 else outer
-        return remote(ref, ref, g_send.at[way, b], g_recv.at[b, p], target)
+        return remote(ref, ref, g_send.at[way, b], g_recv.at[b, p, part], target)
+
+    def tok_take(way, r, p, onward):
+        for part in range(parts):
+            tok(way, r, p, part).wait_recv()
+
+            @pl.when(onward)
+            def _():
+                tok(way, r, p, part).start()
 
     def tok_sent(way, r, count):
         b = blk(r)
         ref = got.at[b, pl.ds(0, count)]
         target = inner if way == 0 else outer
-        remote(ref, ref, g_send.at[way, b], g_recv.at[b, 0], target).wait_send()
+        remote(ref, ref, g_send.at[way, b], g_recv.at[b, 0, 0], target).wait_send()
 
     far_rows = w_far.shape[1] // seats
     far_base = near * deep
@@ -724,11 +730,10 @@
                 part_copy(r, kind).start()
 
     halves = wo_recv.shape[2]
-    half_rows = wo_ref.shape[2] // halves
 
     def wo_copy(way, r, cut, half):
         b = blk(r)
-        ref = wo_ref.at[b, cut, pl.ds(half * half_rows, half_rows)]
+        ref = wo_ref.at[b, cut * halves + half]
         target = inner if way == 0 else outer
         return remote(ref, ref, wo_send.at[way, b], wo_recv.at[b, cut, half], target)
 
@@ -739,7 +744,7 @@
 
     along = [(0, r, cut) for cut in range(cuts) for r in (1, 0)]
     back = [(1, r, cut) for cut in range(cuts) for r in (2, 3)]
-    early = 2
+    early = 3
 
     def wo_next(way, r, cut):
         for half in range(halves):
@@ -761,9 +766,11 @@
         ref, slot = kv_ref.at[b], kv_in.at[1, b]
         return remote(ref, slot, kv_send.at[1], kv_recv.at[1], along_x)
 
-    def kv_relay():
-        slot = 2 * (1 - core)
-        return remote(kv_in.at[1], kv_in.at[slot], kv_send.at[2], kv_recv.at[slot], partner)
+    def kv_cross(b):
+        at = 2 * (1 - core)
+        ref, slot = kv_ref.at[b], kv_in.at[at, b]
+        target = place(across[1], 1 - core)
+        return remote(ref, slot, kv_send.at[2], kv_recv.at[at], target)
 
     def kv_slot(slot):
         return remote(kv_ref, kv_in.at[slot], kv_send.at[slot], kv_recv.at[slot], partner)
@@ -792,12 +799,12 @@
         @pl.when(tract < 2)
         def _():
             kv_far(blk(r)).start()
+            kv_cross(blk(r)).start()
 
         @pl.when(core == 0)
         def _():
             kv_near(blk(r)).start()
 
-    acc_ref[...] = jnp.zeros_like(acc_ref)
     own_load.wait()
     power = jnp.zeros((rows, 1), jnp.float32)
     for p in range(pieces):
@@ -815,15 +822,17 @@
     def send_own(p):
         @pl.when(is_end)
         def _():
-            tok(0, 0, p).start()
+            for part in range(parts):
+                tok(0, 0, p, part).start()
             if p == 0:
                 far_first(0).start()
 
         @pl.when(is_helper)
         def _():
-            tok(0, 1, p).start()
-            if p < near:
-                tok(1, 1, p).start()
+            for part in range(parts):
+                tok(0, 1, p, part).start()
+                if p < near:
+                    tok(1, 1, p, part).start()
 
     for p in range(pieces):
         tokens = raw[:, p * deep : (p + 1) * deep].astype(jnp.float32)
@@ -832,12 +841,14 @@
         if p:
             send_own(p - 1)
     send_own(pieces - 1)
+    acc_ref[...] = jnp.zeros_like(acc_ref)
+    gate_ref[...] = table_ref[2, pl.ds(level, 1), :]
 
     @pl.when(is_end)
     def _():
+        wq_load.wait()
         @pl.loop(0, pieces)
         def _(p):
-            wq_load(p).wait()
             accumulate((0,), p)
 
         wo_loaded()
@@ -849,7 +860,7 @@
 
             @pl.loop(0, near)
             def _(p):
-                tok(0, r, p).wait_recv()
+                tok_take(0, r, p, False)
                 accumulate((r,), p)
 
         for r in (1, 2):
@@ -860,7 +871,7 @@
 
         @pl.loop(0, near)
         def _(p):
-            tok(0, 3, p).wait_recv()
+            tok_take(0, 3, p, False)
             accumulate((3,), p)
 
         for kind in (1, 2):
@@ -874,19 +885,13 @@
     @pl.when(is_helper)
     def _():
         def pass_on(p):
-            tok(0, 0, p).wait_recv()
-            tok(0, 0, p).start()
+            tok_take(0, 0, p, True)
             accumulate((0,), p)
 
+        wq_load.wait()
         @pl.loop(0, pieces)
         def _(p):
-            wq_load(p).wait()
-            tok(1, 2, p).wait_recv()
-
-            @pl.when(p < near)
-            def _():
-                tok(1, 2, p).start()
-
+            tok_take(1, 2, p, p < near)
             accumulate((1, 2), p)
             for at, kind in ((1, 1), (3, 2), (7, 0)):
 
@@ -920,16 +925,11 @@
             def _():
                 pass_on(p + 2)
 
+            tok_take(1, 3, p, p < near)
+
             @pl.when(p == pieces - 1)
             def _():
-                far_ready(0)
-                far_part((1, 2), (0,))
-
-            tok(1, 3, p).wait_recv()
-
-            @pl.when(p < near)
-            def _():
-                tok(1, 3, p).start()
+                far_part((3,), (1, 2))
 
             accumulate((3,), p)
 
@@ -958,16 +958,26 @@
                 settle(0, (1, 2, 0))
                 share(0)
 
+            @pl.when(p == 6)
+            def _():
+                wo_next(*along[0])
+
             @pl.when(p == 5)
             def _():
                 far_hand_y(0)
 
-        far_part((3,), (1, 2, 0))
         settle(3, (1, 2))
         share(3)
+        far_ready(0)
+        far_part((1, 2, 3), (0,))
         settle(3, (0,))
-        for way, r, cut in along[:early]:
-            wo_next(way, r, cut)
+        wo_next(*along[1])
+
+        @pl.when(tract >= 2)
+        def _():
+            for move in along[2:early]:
+                wo_next(*move)
+
 
     tokens_here = n * rows
     heads_here = q_ref.shape[2] // HD
@@ -1009,22 +1019,16 @@
 
     attend(kv_ref, None)
 
-    @pl.when(tract >= 2)
-    def _():
-        kv_slot(1).wait_recv()
-        kv_relay().start()
-
-    for ahead in (2, 1, 3):
-        if ahead == 3:
-
-            @pl.when(is_helper)
+    for ahead in (1, 2, 3):
+        if ahead == 2:
+
+            @pl.when(is_helper & (tract >= 2))
             def _():
                 wo_next(*back[0])
 
         @pl.when(tract >= ahead)
         def _():
-            if ahead != 2:
-                kv_slot(ahead - 1).wait_recv()
+            kv_slot(ahead - 1).wait_recv()
             seen = visible_ref[0, lax.max(tract - ahead, 0)] > 0
             attend(kv_in.at[ahead - 1], jnp.where(seen, 0.0, -1e30))
 
@@ -1041,8 +1045,8 @@
             {"head": other},
         )
 
-    for ahead in range(1, n):
-        other = lax.rem(me + ahead, n)
+    line = [blk(jnp.where(is_end, end, help)) for end, help in ((0, 1), (1, 2), (2, 0), (3, 3))]
+    for other in line[1:]:
         att_line(other, me).start()
     att_all[seat, me] = att_ref[me]
 
@@ -1058,10 +1062,13 @@
 
     @pl.when(is_helper)
     def _():
+        @pl.when(tract < 2)
+        def _():
+            for move in along[2:early]:
+                wo_next(*move)
+
         for move in along[early:]:
             wo_next(*move)
-
-    line = [blk(jnp.where(is_end, end, help)) for end, help in ((0, 1), (1, 2), (2, 0), (3, 3))]
 
     for ahead, z in enumerate(line):
         if ahead:
@@ -1069,73 +1076,74 @@
         for by in range(1, chips):
             att_chip(by, z, chip).start()
         att_pass(0, z, core).start()
-        if ahead < 2:
-            wo_moves(back[1 + ahead])
-
-    wo_moves(*back[3:4])
-    for z in line:
+        for late, used in ((0, tract < 2), (1, tract >= 2)):
+
+            @pl.when(is_helper & used)
+            def _():
+                for move in back[ahead + late : min(ahead + late + 1, 3)]:
+                    wo_next(*move)
+
+    for ahead, z in enumerate(line):
         for by in range(1, chips):
             att_chip(by, z, seat_of(by, 0)[0]).wait_recv()
             att_pass(by, z, core).start()
+        if ahead == 2:
+            wo_moves(*back[3:4])
     wo_moves(*back[4:5])
     for by in range(chips):
         att_pass(by, None, 1 - core).wait_recv()
 
-    def out_copy(by, side, source, cut):
+    spans = [(k, 2) for k in range(0, units - 2, 2)] + [(units - 2, 1), (units - 1, 1)]
+
+    def out_copy(by, side, source, at):
         which, lane = seat_of(by, side)
+        span = pl.ds(*spans[at])
         return remote(
-            out_part.at[which * 2 + lane, cut],
-            out_in.at[source, cut],
+            out_part.at[which * 2 + lane, span],
+            out_in.at[source, span],
             o_send.at[which * 2 + lane],
-            o_recv.at[source, cut],
+            o_recv.at[source, at],
             place(which, lane),
         )
 
     heads_wide = wo_ref.shape[2]
 
-    def finish(ref, source, cut):
-        span = pl.ds(pl.multiple_of(source * cols_out + cut * cut_cols, 128), cut_cols)
-        gate = table_ref[2, pl.ds(level, 1), span]
-        done = ref[source, cut].astype(jnp.float32) * gate
-        out_ref[0, :, span] = done.astype(out_ref.dtype)
-
-    def finish_cut(cut):
-        finish(out_part, seat, cut)
+    def finish(ref, source, at):
+        first, count = spans[at]
+        for k in range(first, first + count):
+            span = pl.ds(pl.multiple_of(source * cols_out + k * unit, 128), unit)
+            done = ref[source, k].astype(jnp.float32) * gate_ref[:, span]
+            out_ref[0, :, span] = done.astype(out_ref.dtype)
+
+    for at, (first, count) in enumerate(spans):
+
+        @pl.when(is_end)
+        def _():
+            for r in (1, 2, 3):
+                for k in range(first, first + count):
+                    wo_copy(0, r, k // halves, k % halves).wait_recv()
+
+        total = None
+        for z in range(n):
+            lhs = att_all[:, z].reshape(seats * rows, heads_wide)
+            rhs = jnp.concatenate([wo_ref[z, k] for k in range(first, first + count)], axis=1)
+            made = jnp.dot(lhs, rhs, preferred_element_type=jnp.float32)
+            total = made if total is None else total + made
+        total = total.astype(out_part.dtype).reshape(seats, rows, count * unit)
+        for k in range(count):
+            out_part[:, first + k] = total[:, :, k * unit : (k + 1) * unit]
+        for by, side in others:
+            out_copy(by, side, seat, at).start()
+        if at == max(0, len(spans) - 3):
+            wo_moves(*back[5:])
+
+    for at in range(len(spans)):
+        finish(out_part, seat, at)
         for by, side in reversed(others):
             which, lane = seat_of(by, side)
             source = which * 2 + lane
-            out_copy(by, side, source, cut).wait_recv()
-            finish(out_in, source, cut)
-
-    for cut in range(cuts):
-
-        @pl.when(is_end)
-        def _():
-            if cut == 2:
-                finish_cut(0)
-            for r in (1, 2, 3):
-                for half in range(halves):
-                    wo_copy(0, r, cut, half).wait_recv()
-
-        total = None
-        for z in range(n):
-            lhs = att_all[:, z].reshape(seats * rows, heads_wide)
-            made = jnp.dot(lhs, wo_ref[z, cut], preferred_element_type=jnp.float32)
-            total = made if total is None else total + made
-        out_part[:, cut] = total.astype(out_part.dtype).reshape(seats, rows, cut_cols)
-        for by, side in others:
-            out_copy(by, side, seat, cut).start()
-        if cut == 0:
-            wo_moves(*back[5:])
-
-    for cut in range(cuts):
-        if cut == 0 and cuts > 2:
-
-            @pl.when(is_helper)
-            def _():
-                finish_cut(0)
-        else:
-            finish_cut(cut)
+            out_copy(by, side, source, at).wait_recv()
+            finish(out_in, source, at)
 
     for by, side in others:
         which, lane = seat_of(by, side)
@@ -1148,7 +1156,7 @@
         att_pass(by, None, core).wait_send()
     for ahead in range(1, n):
         att_line(lax.rem(me + ahead, n), me).wait_send()
-    for slot, used in ((0, core == 0), (1, tract < 2), (2, tract >= 2)):
+    for slot, used in ((0, core == 0), (1, tract < 2), (2, tract < 2)):
 
         @pl.when(used)
         def _():
@@ -1214,7 +1222,7 @@
     seats = tracts * reps
     chips = seats // 2
     deep = width // PIECES
-    cuts = width // seats // 256
+    units = width // seats // 128
     vmem = pl.BlockSpec(memory_space=pltpu.VMEM)
     hbm = pl.BlockSpec(memory_space=pltpu.HBM)
     smem = pl.BlockSpec(memory_space=pltpu.SMEM)
@@ -1227,11 +1235,12 @@
         out_specs=vmem,
         scratch_shapes=[
             pltpu.VMEM((3, *modulation.shape[::2]), jnp.float32),
+            pltpu.VMEM((1, width), jnp.float32),
             pltpu.VMEM((rows, width), half),
             pltpu.VMEM((n, PIECES, rows, deep), half),
             pltpu.VMEM((3, width, cols), half),
             pltpu.VMEM((3, (PIECES - NEAR) * deep, cols), half),
-            pltpu.VMEM((n, cuts, w_out.shape[0], 256), half),
+            pltpu.VMEM((n, units, w_out.shape[0], 128), half),
             pltpu.VMEM((n, 3, rows, cols), jnp.float32),
             pltpu.VMEM((n, rows, cols), half),
             pltpu.VMEM((n, 2, rows, cols), half),
@@ -1243,28 +1252,27 @@
             pltpu.VMEM((heads_here, 1, n * rows), jnp.float32),
             pltpu.VMEM((heads_here, HD, n * rows), jnp.float32),
             pltpu.VMEM((seats, n, rows, cols), half),
-            pltpu.VMEM((seats, cuts, rows, 256), half),
-            pltpu.VMEM((seats, cuts, rows, 256), half),
-            dma((2,)),
-            dma((PIECES,)),
-            dma((cuts,)),
+            pltpu.VMEM((seats, units, rows, 128), half),
+            pltpu.VMEM((seats, units, rows, 128), half),
+            dma((3,)),
+            dma((units,)),
             dma((2, n)),
-            dma((n, PIECES)),
+            dma((n, PIECES, 2)),
             dma((2 * chips,)),
             dma((2 * chips, 3)),
             dma((n,)),
             dma((n, 3)),
-            dma((tracts,)),
-            dma((tracts,)),
+            dma((3,)),
+            dma((3,)),
             dma((2, n)),
-            dma((n, cuts, 2)),
+            dma((n, units // 2, 2)),
             dma((n,)),
             dma((n,)),
             dma((2 * chips,)),
             dma((chips, n)),
             dma((chips,)),
             dma((seats,)),
-            dma((seats, cuts)),
+            dma((seats, units // 2 + 1)),
         ],
         compiler_params=pltpu.CompilerParams(
             collective_id=0, has_side_effects=True, vmem_limit_bytes=GRANT

time: 76.5 us -> 75.4 us (0.986)
  Pallas kernels: 74.8 us -> 73.7 us
    pallas_call x1, Pallas kernels: 74.8 us -> 73.7 us  [line_body(): pl.pallas_call(functools.partial(line_kernel, n, tracts, reps, PIECES, NE...]
where the time goes in v4:
time: 75.4 us; the launch traced here: 75.3 us
  Pallas kernels  73.7 us (98%)
  local copies, waits for them, and re-layouts  0.88 us (1%)
    pallas_call x1, Pallas kernels, line_body(): pl.pallas_call(functools.partial(line_kernel, n, tracts, reps, PIECES, NE...  73.7 us

profile of v4, /device:TPU:0, one launch (start us, length us, event | category | flops | bytes accessed | tf_op | source)
XLA Modules:
  0.0 75.3 jit_solution(6549893281193659812)
XLA Ops:
  0.7 73.7 %shard_map.64 = bf16[1,64,6144]{2,1,0:T(8,128)(2,1)S(1)} custom-call(bf16[1,64,6144]{2,1,0:T(8,128)(2,1)} %x_ref.1, s32[1]{0:T(128)S(6)} %copy.9.level_ref, s32[1,4]{1,0:T(1,128)} %visible_ref.1, bf16[3,6144,256]{2,1,0:T(8,128)(2,1)} %bitcast.2, bf16[256,6144]{1,0:T(8,128)(2,1)} %out_hbm.1, f32[3,8,6144]{2,1,0:T(8,128)} %bitcast.3), custom_call_target="tpu_custom_call" | custom-call | tf_op jit(solution)/shard_map/pallas_call | solution.py:1231
  74.4 0.9 %copy.8 = bf16[1,64,6144]{2,1,0:T(8,128)(2,1)} copy(bf16[1,64,6144]{2,1,0:T(8,128)(2,1)S(1)} %shard_map.64) | data formatting | bytes 1572864

commit v5 on v4

--- a/solution.py
+++ b/solution.py
@@ -594,27 +594,6 @@
 
     own_load = pltpu.make_async_copy(x_ref.at[0], raw, load_sem.at[0])
     own_load.start()
-    table_load = pltpu.make_async_copy(table_hbm, table_ref, load_sem.at[1])
-    table_load.start()
-    cols_out = width // seats
-    units = wo_ref.shape[1]
-    cuts, unit = units // 2, cols_out // units
-
-    def wo_load(k):
-        start = pl.multiple_of(seat * cols_out + k * unit, 128)
-        src = out_hbm.at[:, pl.ds(start, unit)]
-        return pltpu.make_async_copy(src, wo_ref.at[me, k], wo_sem.at[k])
-
-    def wo_loaded():
-        for k in range(units):
-            wo_load(k).wait()
-
-    wq_load = pltpu.make_async_copy(w_hbm, wq_ref, load_sem.at[2])
-    wq_load.start()
-
-    for k in range(units):
-        wo_load(k).start()
-
     barrier = pltpu.get_barrier_semaphore()
     for ahead in range(1, n):
         other = lax.rem(me + ahead, n)
@@ -622,6 +601,27 @@
     for other in others:
         target = place(*seat_of(*other))
         pl.semaphore_signal(barrier, inc=1, device_id=target, device_id_type=MESH)
+
+    table_load = pltpu.make_async_copy(table_hbm, table_ref, load_sem.at[1])
+    table_load.start()
+    cols_out = width // seats
+    units = wo_ref.shape[1]
+    cuts, unit = units // 2, cols_out // units
+
+    def wo_load(k):
+        start = pl.multiple_of(seat * cols_out + k * unit, 128)
+        src = out_hbm.at[:, pl.ds(start, unit)]
+        return pltpu.make_async_copy(src, wo_ref.at[me, k], wo_sem.at[k])
+
+    def wo_loaded():
+        for k in range(units):
+            wo_load(k).wait()
+
+    wq_load = pltpu.make_async_copy(w_hbm, wq_ref, load_sem.at[2])
+    wq_load.start()
+
+    for k in range(units):
+        wo_load(k).start()
 
     level = level_ref[0]
 
@@ -641,25 +641,34 @@
     parts = g_recv.shape[2]
     part_rows = rows // parts
 
-    def tok(way, r, p, part):
+    def row_there(way, r, onward):
+        if way == 1:
+            return r - 1
+        return 1 if r == 1 else 2 if onward else 0
+
+    def row_here(r):
+        return max(r - 1, 0)
+
+    def tok(way, r, p, part, row):
         b = blk(r)
         ref = got.at[b, p, pl.ds(part * part_rows, part_rows)]
         target = inner if way == 0 else outer
-        return remote(ref, ref, g_send.at[way, b], g_recv.at[b, p, part], target)
+        return remote(ref, ref, g_send.at[way, b], g_recv.at[row, p, part], target)
 
     def tok_take(way, r, p, onward):
         for part in range(parts):
-            tok(way, r, p, part).wait_recv()
-
-            @pl.when(onward)
-            def _():
-                tok(way, r, p, part).start()
+            tok(way, r, p, part, row_here(r)).wait_recv()
+            if onward is not None:
+
+                @pl.when(onward)
+                def _():
+                    tok(way, r, p, part, row_there(way, r, True)).start()
 
     def tok_sent(way, r, count):
         b = blk(r)
         ref = got.at[b, pl.ds(0, count)]
         target = inner if way == 0 else outer
-        remote(ref, ref, g_send.at[way, b], g_recv.at[b, 0, 0], target).wait_send()
+        remote(ref, ref, g_send.at[way, b], g_recv.at[0, 0, 0], target).wait_send()
 
     far_rows = w_far.shape[1] // seats
     far_base = near * deep
@@ -731,16 +740,16 @@
 
     halves = wo_recv.shape[2]
 
-    def wo_copy(way, r, cut, half):
+    def wo_copy(way, r, cut, half, row):
         b = blk(r)
         ref = wo_ref.at[b, cut * halves + half]
         target = inner if way == 0 else outer
-        return remote(ref, ref, wo_send.at[way, b], wo_recv.at[b, cut, half], target)
+        return remote(ref, ref, wo_send.at[way, b], wo_recv.at[row, cut, half], target)
 
     def wo_start(way, r, which):
         for cut in which:
             for half in range(halves):
-                wo_copy(way, r, cut, half).start()
+                wo_copy(way, r, cut, half, row_there(way, r, False)).start()
 
     along = [(0, r, cut) for cut in range(cuts) for r in (1, 0)]
     back = [(1, r, cut) for cut in range(cuts) for r in (2, 3)]
@@ -749,8 +758,8 @@
     def wo_next(way, r, cut):
         for half in range(halves):
             if r != 1:
-                wo_copy(way, r, cut, half).wait_recv()
-            wo_copy(way, r, cut, half).start()
+                wo_copy(way, r, cut, half, row_here(r)).wait_recv()
+            wo_copy(way, r, cut, half, row_there(way, r, True)).start()
 
     def wo_moves(*moves):
         @pl.when(is_helper)
@@ -758,17 +767,17 @@
             for move in moves:
                 wo_next(*move)
 
-    def kv_near(b):
-        ref, slot = kv_ref.at[b], kv_in.at[0, b]
+    def kv_near(b, kinds):
+        ref, slot = kv_ref.at[b, kinds], kv_in.at[0, b, kinds]
         return remote(ref, slot, kv_send.at[0], kv_recv.at[0], partner)
 
-    def kv_far(b):
-        ref, slot = kv_ref.at[b], kv_in.at[1, b]
+    def kv_far(b, kinds):
+        ref, slot = kv_ref.at[b, kinds], kv_in.at[1, b, kinds]
         return remote(ref, slot, kv_send.at[1], kv_recv.at[1], along_x)
 
-    def kv_cross(b):
+    def kv_cross(b, kinds):
         at = 2 * (1 - core)
-        ref, slot = kv_ref.at[b], kv_in.at[at, b]
+        ref, slot = kv_ref.at[b, kinds], kv_in.at[at, b, kinds]
         target = place(across[1], 1 - core)
         return remote(ref, slot, kv_send.at[2], kv_recv.at[at], target)
 
@@ -795,15 +804,17 @@
             else:
                 kv_ref[b, kind - 1] = made
 
-    def share(r):
+    def share(r, first=0, count=2):
+        kinds = pl.ds(first, count)
+
         @pl.when(tract < 2)
         def _():
-            kv_far(blk(r)).start()
-            kv_cross(blk(r)).start()
+            kv_far(blk(r), kinds).start()
+            kv_cross(blk(r), kinds).start()
 
         @pl.when(core == 0)
         def _():
-            kv_near(blk(r)).start()
+            kv_near(blk(r), kinds).start()
 
     own_load.wait()
     power = jnp.zeros((rows, 1), jnp.float32)
@@ -823,16 +834,16 @@
         @pl.when(is_end)
         def _():
             for part in range(parts):
-                tok(0, 0, p, part).start()
+                tok(0, 0, p, part, 0).start()
             if p == 0:
                 far_first(0).start()
 
         @pl.when(is_helper)
         def _():
             for part in range(parts):
-                tok(0, 1, p, part).start()
+                tok(0, 1, p, part, 1).start()
                 if p < near:
-                    tok(1, 1, p, part).start()
+                    tok(1, 1, p, part, 0).start()
 
     for p in range(pieces):
         tokens = raw[:, p * deep : (p + 1) * deep].astype(jnp.float32)
@@ -860,18 +871,18 @@
 
             @pl.loop(0, near)
             def _(p):
-                tok_take(0, r, p, False)
+                tok_take(0, r, p, None)
                 accumulate((r,), p)
 
-        for r in (1, 2):
-            for kind in (1, 2):
+        for kind in (1, 2):
+            for r in (1, 2):
                 part_copy(r, kind).wait_recv()
-            settle(r, (1, 2), True)
-            share(r)
+                settle(r, (kind,), True)
+                share(r, kind - 1, 1)
 
         @pl.loop(0, near)
         def _(p):
-            tok_take(0, 3, p, False)
+            tok_take(0, 3, p, None)
             accumulate((3,), p)
 
         for kind in (1, 2):
@@ -1052,7 +1063,7 @@
 
     def att_chip(by, z, which):
         ref = att_all.at[which * 2 + core] if z is None else att_all.at[which * 2 + core, z]
-        at = a_recv.at[by, 0 if z is None else z]
+        at = a_recv.at[by - 1, 0 if z is None else z]
         return remote(ref, ref, a_send.at[by], at, place(seat_of(by, 0)[0], core))
 
     def att_pass(by, z, side):
@@ -1121,19 +1132,28 @@
         def _():
             for r in (1, 2, 3):
                 for k in range(first, first + count):
-                    wo_copy(0, r, k // halves, k % halves).wait_recv()
-
-        total = None
-        for z in range(n):
-            lhs = att_all[:, z].reshape(seats * rows, heads_wide)
-            rhs = jnp.concatenate([wo_ref[z, k] for k in range(first, first + count)], axis=1)
-            made = jnp.dot(lhs, rhs, preferred_element_type=jnp.float32)
-            total = made if total is None else total + made
-        total = total.astype(out_part.dtype).reshape(seats, rows, count * unit)
-        for k in range(count):
-            out_part[:, first + k] = total[:, :, k * unit : (k + 1) * unit]
-        for by, side in others:
-            out_copy(by, side, seat, at).start()
+                    wo_copy(0, r, k // halves, k % halves, r - 1).wait_recv()
+
+        rhs = [
+            jnp.concatenate([wo_ref[z, k] for k in range(first, first + count)], axis=1)
+            for z in range(n)
+        ]
+        for pair in ((1, 2), (3, 0)):
+            firsts = [seat_of(by, 0)[0] * 2 for by in pair]
+            total = None
+            for z in range(n):
+                lhs = jnp.concatenate([att_all[pl.ds(q, 2), z] for q in firsts], axis=0)
+                lhs = lhs.reshape(4 * rows, heads_wide)
+                made = jnp.dot(lhs, rhs[z], preferred_element_type=jnp.float32)
+                total = made if total is None else total + made
+            total = total.astype(out_part.dtype).reshape(4, rows, count * unit)
+            for j, q in enumerate(firsts):
+                for k in range(count):
+                    columns = slice(k * unit, (k + 1) * unit)
+                    out_part[pl.ds(q, 2), first + k] = total[2 * j : 2 * j + 2, :, columns]
+            for by, side in others:
+                if by in pair:
+                    out_copy(by, side, seat, at).start()
         if at == max(0, len(spans) - 3):
             wo_moves(*back[5:])
 
@@ -1168,7 +1188,7 @@
 
     def wo_sent(way, r):
         ref = wo_ref.at[blk(r)]
-        sems = wo_send.at[way, blk(r)], wo_recv.at[blk(r), 0, 0]
+        sems = wo_send.at[way, blk(r)], wo_recv.at[0, 0, 0]
         remote(ref, ref, *sems, partner).wait_send()
 
     @pl.when(is_end)
@@ -1257,7 +1277,7 @@
             dma((3,)),
             dma((units,)),
             dma((2, n)),
-            dma((n, PIECES, 2)),
+            dma((n - 1, PIECES, 2)),
             dma((2 * chips,)),
             dma((2 * chips, 3)),
             dma((n,)),
@@ -1265,11 +1285,11 @@
             dma((3,)),
             dma((3,)),
             dma((2, n)),
-            dma((n, units // 2, 2)),
+            dma((n - 1, units // 2, 2)),
             dma((n,)),
             dma((n,)),
             dma((2 * chips,)),
-            dma((chips, n)),
+            dma((chips - 1, n)),
             dma((chips,)),
             dma((seats,)),
             dma((seats, units // 2 + 1)),

time: 75.4 us -> 74.9 us (level)
  no operation moved by 1% of the time
where the time goes in v5:
time: 74.9 us; the launch traced here: 74.7 us
  Pallas kernels  73.2 us (98%)
  local copies, waits for them, and re-layouts  0.88 us (1%)
    pallas_call x1, Pallas kernels, line_body(): pl.pallas_call(functools.partial(line_kernel, n, tracts, reps, PIECES, NE...  73.2 us

profile of v5, /device:TPU:0, one launch (start us, length us, event | category | flops | bytes accessed | tf_op | source)
XLA Modules:
  0.0 74.7 jit_solution(13692700115943681966)
XLA Ops:
  0.7 73.2 %shard_map.64 = bf16[1,64,6144]{2,1,0:T(8,128)(2,1)S(1)} custom-call(bf16[1,64,6144]{2,1,0:T(8,128)(2,1)} %x_ref.1, s32[1]{0:T(128)S(6)} %copy.9.level_ref, s32[1,4]{1,0:T(1,128)} %visible_ref.1, bf16[3,6144,256]{2,1,0:T(8,128)(2,1)} %bitcast.2, bf16[256,6144]{1,0:T(8,128)(2,1)} %out_hbm.1, f32[3,8,6144]{2,1,0:T(8,128)} %bitcast.3), custom_call_target="tpu_custom_call" | custom-call | tf_op jit(solution)/shard_map/pallas_call | solution.py:1251
  73.9 0.9 %copy.8 = bf16[1,64,6144]{2,1,0:T(8,128)(2,1)} copy(bf16[1,64,6144]{2,1,0:T(8,128)(2,1)S(1)} %shard_map.64) | data formatting | bytes 1572864

commit v6 on v5

--- a/solution.py
+++ b/solution.py
@@ -653,7 +653,7 @@
         b = blk(r)
         ref = got.at[b, p, pl.ds(part * part_rows, part_rows)]
         target = inner if way == 0 else outer
-        return remote(ref, ref, g_send.at[way, b], g_recv.at[row, p, part], target)
+        return remote(ref, ref, g_send.at[way], g_recv.at[row, p, part], target)
 
     def tok_take(way, r, p, onward):
         for part in range(parts):
@@ -664,11 +664,9 @@
                 def _():
                     tok(way, r, p, part, row_there(way, r, True)).start()
 
-    def tok_sent(way, r, count):
-        b = blk(r)
-        ref = got.at[b, pl.ds(0, count)]
-        target = inner if way == 0 else outer
-        remote(ref, ref, g_send.at[way, b], g_recv.at[0, 0, 0], target).wait_send()
+    def tok_sent(way, blocks, count):
+        ref = got.at[pl.ds(0, blocks), pl.ds(0, count)]
+        remote(ref, ref, g_send.at[way], g_recv.at[0, 0, 0], partner).wait_send()
 
     far_rows = w_far.shape[1] // seats
     far_base = near * deep
@@ -744,7 +742,7 @@
         b = blk(r)
         ref = wo_ref.at[b, cut * halves + half]
         target = inner if way == 0 else outer
-        return remote(ref, ref, wo_send.at[way, b], wo_recv.at[row, cut, half], target)
+        return remote(ref, ref, wo_send.at[way], wo_recv.at[row, cut, half], target)
 
     def wo_start(way, r, which):
         for cut in which:
@@ -1051,7 +1049,7 @@
         return remote(
             att_ref.at[other],
             att_all.at[seat, source],
-            z_send.at[other],
+            z_send.at[0],
             z_recv.at[source],
             {"head": other},
         )
@@ -1112,7 +1110,7 @@
         return remote(
             out_part.at[which * 2 + lane, span],
             out_in.at[source, span],
-            o_send.at[which * 2 + lane],
+            o_send.at[0],
             o_recv.at[source, at],
             place(which, lane),
         )
@@ -1165,17 +1163,15 @@
             out_copy(by, side, source, at).wait_recv()
             finish(out_in, source, at)
 
-    for by, side in others:
-        which, lane = seat_of(by, side)
-        to = which * 2 + lane
-        sems = o_send.at[to], o_recv.at[seat, 0]
-        remote(out_part.at[to], out_in.at[seat], *sems, partner).wait_send()
+    peers = pl.ds(0, seats - 1)
+    sems = o_send.at[0], o_recv.at[seat, 0]
+    remote(out_part.at[peers], out_in.at[peers], *sems, partner).wait_send()
     for by in range(chips):
         if by:
             att_chip(by, None, chip).wait_send()
         att_pass(by, None, core).wait_send()
-    for ahead in range(1, n):
-        att_line(lax.rem(me + ahead, n), me).wait_send()
+    ref = att_ref.at[pl.ds(0, n - 1)]
+    remote(ref, ref, z_send.at[0], z_recv.at[me], partner).wait_send()
     for slot, used in ((0, core == 0), (1, tract < 2), (2, tract < 2)):
 
         @pl.when(used)
@@ -1186,16 +1182,16 @@
         ref = w_far.at[:, far_span(which, core)]
         remote(ref, ref, f_send.at[where], f_recv.at[where, 0], partner).wait_send()
 
-    def wo_sent(way, r):
-        ref = wo_ref.at[blk(r)]
-        sems = wo_send.at[way, blk(r)], wo_recv.at[0, 0, 0]
+    def wo_sent(way, blocks):
+        ref = wo_ref.at[pl.ds(0, blocks)]
+        sems = wo_send.at[way], wo_recv.at[0, 0, 0]
         remote(ref, ref, *sems, partner).wait_send()
 
     @pl.when(is_end)
     def _():
         far_sent(0, chip)
-        tok_sent(0, 0, pieces)
-        wo_sent(0, 0)
+        tok_sent(0, 1, pieces)
+        wo_sent(0, 1)
 
     @pl.when(is_helper)
     def _():
@@ -1207,11 +1203,10 @@
             ref = part_ref.at[blk(r)]
             sems = p_send.at[blk(r)], p_recv.at[blk(r), 0]
             remote(ref, ref, *sems, partner).wait_send()
-            tok_sent(1, r, near)
-            wo_sent(1, r)
-        for r in (0, 1):
-            tok_sent(0, r, pieces)
-            wo_sent(0, r)
+        tok_sent(1, 3, near)
+        wo_sent(1, 3)
+        tok_sent(0, 2, pieces)
+        wo_sent(0, 2)
 
 
 PIECES = 8
@@ -1276,7 +1271,7 @@
             pltpu.VMEM((seats, units, rows, 128), half),
             dma((3,)),
             dma((units,)),
-            dma((2, n)),
+            dma((2,)),
             dma((n - 1, PIECES, 2)),
             dma((2 * chips,)),
             dma((2 * chips, 3)),
@@ -1284,14 +1279,14 @@
             dma((n, 3)),
             dma((3,)),
             dma((3,)),
-            dma((2, n)),
+            dma((2,)),
             dma((n - 1, units // 2, 2)),
-            dma((n,)),
+            dma((1,)),
             dma((n,)),
             dma((2 * chips,)),
             dma((chips - 1, n)),
             dma((chips,)),
-            dma((seats,)),
+            dma((1,)),
             dma((seats, units // 2 + 1)),
         ],
         compiler_params=pltpu.CompilerParams(

time: 74.9 us -> 74.7 us (level)
  no operation moved by 1% of the time
where the time goes in v6:
time: 74.7 us; the launch traced here: 74.5 us
  Pallas kernels  73 us (98%)
  local copies, waits for them, and re-layouts  0.88 us (1%)
    pallas_call x1, Pallas kernels, line_body(): pl.pallas_call(functools.partial(line_kernel, n, tracts, reps, PIECES, NE...  73 us

profile of v6, /device:TPU:0, one launch (start us, length us, event | category | flops | bytes accessed | tf_op | source)
XLA Modules:
  0.0 74.5 jit_solution(13396730630260759207)
XLA Ops:
  0.7 73.0 %shard_map.64 = bf16[1,64,6144]{2,1,0:T(8,128)(2,1)S(1)} custom-call(bf16[1,64,6144]{2,1,0:T(8,128)(2,1)} %x_ref.1, s32[1]{0:T(128)S(6)} %copy.9.level_ref, s32[1,4]{1,0:T(1,128)} %visible_ref.1, bf16[3,6144,256]{2,1,0:T(8,128)(2,1)} %bitcast.2, bf16[256,6144]{1,0:T(8,128)(2,1)} %out_hbm.1, f32[3,8,6144]{2,1,0:T(8,128)} %bitcast.3), custom_call_target="tpu_custom_call" | custom-call | tf_op jit(solution)/shard_map/pallas_call | solution.py:1246
  73.6 0.9 %copy.8 = bf16[1,64,6144]{2,1,0:T(8,128)(2,1)} copy(bf16[1,64,6144]{2,1,0:T(8,128)(2,1)S(1)} %shard_map.64) | data formatting | bytes 1572864

commit v7 on v6

--- a/solution.py
+++ b/solution.py
@@ -1062,12 +1062,12 @@
     def att_chip(by, z, which):
         ref = att_all.at[which * 2 + core] if z is None else att_all.at[which * 2 + core, z]
         at = a_recv.at[by - 1, 0 if z is None else z]
-        return remote(ref, ref, a_send.at[by], at, place(seat_of(by, 0)[0], core))
+        return remote(ref, ref, a_send.at[0], at, place(seat_of(by, 0)[0], core))
 
     def att_pass(by, z, side):
         owner = seat_of(by, 0)[0] * 2 + side
         ref = att_all.at[owner] if z is None else att_all.at[owner, z]
-        return remote(ref, ref, a_send.at[chips + by], b_recv.at[by], partner)
+        return remote(ref, ref, a_send.at[1], b_recv.at[0], partner)
 
     @pl.when(is_helper)
     def _():
@@ -1099,8 +1099,11 @@
         if ahead == 2:
             wo_moves(*back[3:4])
     wo_moves(*back[4:5])
-    for by in range(chips):
-        att_pass(by, None, 1 - core).wait_recv()
+    def att_passes(count):
+        ref = att_all.at[pl.ds(0, count)]
+        return remote(ref, ref, a_send.at[1], b_recv.at[0], partner)
+
+    att_passes(chips).wait_recv()
 
     spans = [(k, 2) for k in range(0, units - 2, 2)] + [(units - 2, 1), (units - 1, 1)]
 
@@ -1166,10 +1169,9 @@
     peers = pl.ds(0, seats - 1)
     sems = o_send.at[0], o_recv.at[seat, 0]
     remote(out_part.at[peers], out_in.at[peers], *sems, partner).wait_send()
-    for by in range(chips):
-        if by:
-            att_chip(by, None, chip).wait_send()
-        att_pass(by, None, core).wait_send()
+    ref = att_all.at[pl.ds(0, chips - 1)]
+    remote(ref, ref, a_send.at[0], b_recv.at[0], partner).wait_send()
+    att_passes(chips).wait_send()
     ref = att_ref.at[pl.ds(0, n - 1)]
     remote(ref, ref, z_send.at[0], z_recv.at[me], partner).wait_send()
     for slot, used in ((0, core == 0), (1, tract < 2), (2, tract < 2)):
@@ -1283,9 +1285,9 @@
             dma((n - 1, units // 2, 2)),
             dma((1,)),
             dma((n,)),
-            dma((2 * chips,)),
+            dma((2,)),
             dma((chips - 1, n)),
-            dma((chips,)),
+            dma((1,)),
             dma((1,)),
             dma((seats, units // 2 + 1)),
         ],

time: 74.7 us -> 74.6 us (level)
  no operation moved by 1% of the time
where the time goes in v7:
time: 74.6 us; the launch traced here: 74.4 us
  Pallas kernels  72.9 us (98%)
  local copies, waits for them, and re-layouts  0.88 us (1%)
    pallas_call x1, Pallas kernels, line_body(): pl.pallas_call(functools.partial(line_kernel, n, tracts, reps, PIECES, NE...  72.9 us

profile of v7, /device:TPU:0, one launch (start us, length us, event | category | flops | bytes accessed | tf_op | source)
XLA Modules:
  0.0 74.4 jit_solution(8912403983188088319)
XLA Ops:
  0.7 72.9 %shard_map.64 = bf16[1,64,6144]{2,1,0:T(8,128)(2,1)S(1)} custom-call(bf16[1,64,6144]{2,1,0:T(8,128)(2,1)} %x_ref.1, s32[1]{0:T(128)S(6)} %copy.9.level_ref, s32[1,4]{1,0:T(1,128)} %visible_ref.1, bf16[3,6144,256]{2,1,0:T(8,128)(2,1)} %bitcast.2, bf16[256,6144]{1,0:T(8,128)(2,1)} %out_hbm.1, f32[3,8,6144]{2,1,0:T(8,128)} %bitcast.3), custom_call_target="tpu_custom_call" | custom-call | tf_op jit(solution)/shard_map/pallas_call | solution.py:1248
  73.5 0.9 %copy.8 = bf16[1,64,6144]{2,1,0:T(8,128)(2,1)} copy(bf16[1,64,6144]{2,1,0:T(8,128)(2,1)S(1)} %shard_map.64) | data formatting | bytes 1572864
